TPU v7x, 32 devices: a whole 2x2x4 slice. The times are simulated.
32 devices in a mesh: leaf: 8 (over z, y), sub: 4 (over x, core).
Axes of the slice: x: 2, y: 2, z: 4, core: 2. Of those that a mesh axis runs over, the one named last changes fastest.
Arguments:
- points: float32 [3, 32768], P(None, ('leaf', 'sub')), may hold values from 0 to 4
- order: int32 [32, 1024], P(('leaf', 'sub')), may hold values from 0 to 1023, each once within a row
- counts: int32 [32], P(('leaf', 'sub')), may hold values from 1 to 1024, 24576 in all
- basis: float32 [32768, 640], P(('leaf', 'sub')), may hold values from -0.1875 to 0.1875
- right_side: float32 [32768, 128], P(('leaf', 'sub')), may hold values from -6 to 6
- coupling: float32 [5, 256, 256], replicated, may hold values from -0.375 to 0.375
Outputs:
- solution: float32 [32768, 128], P(('leaf', 'sub'))
Inputs may be any that keep to these rules, and one draw needn't show every extreme that they name: `order`: each row orders the 1024 slots of one leaf, every slot once. `counts`: slots of a leaf at or past its count are padding; some leaf is full.
All inputs are finite; a program needn't handle non-finite values. No bound on the sum of `counts` on one device may be relied on, other than what follows from the above.
Results may differ from a plain program's by a relative error of at most 0.0003.
Values sent between devices are 32-bit elements; how exact they have to be, the bound alone decides.
No kernel may reach another device: no remote copies, remote signals or barrier semaphores. Data moves between devices by JAX's collectives and lax.ppermute only.
A program may use at most 128 MiB of HBM per device.

v0:
```python
import jax
import jax.numpy as jnp
from jax import lax
from jax.sharding import PartitionSpec as P

R = 128


GAMMA_RATE = 2.0
NUGGET_VALUE = 1.0


def swapped(shard, axis, stride):
    return lax.ppermute(shard, axis, [(i, i ^ 1 << stride) for i in range(lax.axis_size(axis))])


def leaf_solve(coords, ordering, count, basis_rows, rhs_rows):
    ordered = coords[:, ordering]
    live_mask = (jnp.arange(coords.shape[1]) < count).astype(jnp.float32)
    offsets = ordered[:, :, None] - ordered[:, None, :]
    distance = jnp.sum(offsets * offsets, axis=0)
    kernel = jnp.exp(-GAMMA_RATE * distance) * live_mask[:, None] * live_mask[None, :]
    kernel = kernel + NUGGET_VALUE * jnp.eye(coords.shape[1], dtype=jnp.float32)
    lower_tri = jnp.linalg.cholesky(kernel)
    stacked = jnp.concatenate([basis_rows, rhs_rows], axis=1) * live_mask[:, None]
    solved = jax.scipy.linalg.cho_solve((lower_tri, True), stacked)
    return (solved, stacked[:, : basis_rows.shape[1]])


def couple(first_sums, second_sums, factor):
    upper_half = factor[:R]
    lower_half = factor[R:]
    highest = lax.Precision.HIGHEST
    first_block = first_sums[:, :R]
    second_block = second_sums[:, :R]
    coupled = jnp.eye(2 * R, dtype=jnp.float32)
    coupled = coupled + jnp.dot(
        upper_half.T, jnp.dot(first_block, upper_half, precision=highest), precision=highest
    )
    coupled = coupled + jnp.dot(
        lower_half.T, jnp.dot(second_block, lower_half, precision=highest), precision=highest
    )
    coupled = 0.5 * (coupled + coupled.T)
    forcing = jnp.dot(upper_half.T, first_sums, precision=highest) + jnp.dot(
        lower_half.T, second_sums, precision=highest
    )
    lower_tri = jnp.linalg.cholesky(coupled)
    solved_coef = jax.scipy.linalg.cho_solve((lower_tri, True), forcing)
    return jnp.dot(factor, solved_coef, precision=highest)


def pair_swap(payload, bit_index, sub_bits):
    if bit_index < sub_bits:
        return swapped(payload, "sub", bit_index)
    return swapped(payload, "leaf", bit_index - sub_bits)


def shards(points, order, counts, basis, right_side, coupling):
    highest = lax.Precision.HIGHEST
    solved, masked = leaf_solve(points, order[0], counts[0], basis, right_side)
    levels = basis.shape[1] // R
    sub_bits = lax.axis_size("sub").bit_length() - 1
    position = lax.axis_index("leaf") * lax.axis_size("sub") + lax.axis_index("sub")
    for tree_level in range(levels):
        col_start = tree_level * R
        own_sums = jnp.einsum(
            "nr,nc->rc",
            masked[:, col_start : col_start + R],
            solved[:, col_start:],
            precision=highest,
        )
        lowest = 0
        if tree_level >= sub_bits:
            lowest = 0
        for bit_index in range(lowest, tree_level):
            own_sums = own_sums + pair_swap(own_sums, bit_index, sub_bits)
        sibling = pair_swap(own_sums, tree_level, sub_bits)
        side_bit = position >> tree_level & 1
        first_sums = jnp.where(side_bit == 0, own_sums, sibling)
        second_sums = jnp.where(side_bit == 0, sibling, own_sums)
        mixed = couple(first_sums, second_sums, coupling[tree_level])
        own_mixed = jnp.where(side_bit == 0, mixed[:R], mixed[R:])
        update = jnp.dot(solved[:, col_start : col_start + R], own_mixed, precision=highest)
        solved = solved.at[:, col_start:].add(-update)
    return solved[:, levels * R :]


def solution(mesh):
    placed = (
        P(None, ("leaf", "sub")),
        P(("leaf", "sub"), None),
        P(("leaf", "sub")),
        P(("leaf", "sub"), None),
        P(("leaf", "sub"), None),
        P(),
    )
    return jax.shard_map(
        shards, mesh=mesh, in_specs=placed, out_specs=P(("leaf", "sub"), None), check_vma=False
    )
```

profile of v0, /device:TPU:0, one launch (start us, length us, event | category | flops | bytes accessed | tf_op | source)
XLA Modules:
  0.0 900.3 jit_solution(7486816521524189942)
XLA Ops:
  30.7 11.7 %cholesky.253 = f32[128,128]{1,0:T(8,128)S(1)} custom-call(f32[128,128]{1,0:T(8,128)S(1)} %cholesky.907), custom_call_target="Cholesky" | custom-call | tf_op jit(solution)/shard_map/jit(cholesky)/cholesky | solution.py:24
  58.7 11.9 %cholesky.276 = f32[128,128]{1,0:T(8,128)S(1)} custom-call(f32[128,128]{1,0:T(8,128)S(1)} %cholesky.911), custom_call_target="Cholesky" | custom-call | tf_op jit(solution)/shard_map/jit(cholesky)/cholesky | solution.py:24
  84.4 11.7 %cholesky.301 = f32[128,128]{1,0:T(8,128)S(1)} custom-call(f32[128,128]{1,0:T(8,128)S(1)} %cholesky.916), custom_call_target="Cholesky" | custom-call | tf_op jit(solution)/shard_map/jit(cholesky)/cholesky | solution.py:24
  110.8 12.1 %cholesky.543 = f32[128,128]{1,0:T(8,128)S(1)} custom-call(f32[128,128]{1,0:T(8,128)S(1)} %cholesky.921), custom_call_target="Cholesky" | custom-call | tf_op jit(solution)/shard_map/jit(cholesky)/cholesky | solution.py:24
  137.4 11.7 %cholesky.562 = f32[128,128]{1,0:T(8,128)S(1)} custom-call(f32[128,128]{1,0:T(8,128)S(1)} %cholesky.926), custom_call_target="Cholesky" | custom-call | tf_op jit(solution)/shard_map/jit(cholesky)/cholesky | solution.py:24
  163.7 11.7 %cholesky.582 = f32[128,128]{1,0:T(8,128)S(1)} custom-call(f32[128,128]{1,0:T(8,128)S(1)} %cholesky.931), custom_call_target="Cholesky" | custom-call | tf_op jit(solution)/shard_map/jit(cholesky)/cholesky | solution.py:24
  189.5 11.9 %cholesky.602 = f32[128,128]{1,0:T(8,128)S(1)} custom-call(f32[128,128]{1,0:T(8,128)S(1)} %cholesky.936), custom_call_target="Cholesky" | custom-call | tf_op jit(solution)/shard_map/jit(cholesky)/cholesky | solution.py:24
  215.1 11.7 %cholesky.616 = f32[128,128]{1,0:T(8,128)S(1)} custom-call(f32[128,128]{1,0:T(8,128)S(1)} %convolution_subtract_fusion.28), custom_call_target="Cholesky" | custom-call | tf_op jit(solution)/shard_map/jit(cholesky)/cholesky | solution.py:24
  238.6 22.8 %while.12 = (s32[]{:T(128)}, f32[1024,1024]{1,0:T(8,128)}, s32[8,2]{0,1:T(2,128)S(1)}, f32[8,128,128]{2,1,0:T(8,128)S(1)}, s32[]{:T(128)}) while((s32[]{:T(128)}, f32[1024,1024]{1,0:T(8,128)}, s32[8,2]{0,1:T(2,128)S(1)}, f32[8,128,128]{2,1,0:T(8,128)S(1)}, s32[]{:T(128)}) %tuple.171), condition=%wide.while_cond.5, body=%wide.while_body.5.sunk | while | flops 2 | bytes 131181 | solution.py:26
  261.4 79.6 %custom-call.109 = f32[8,128,128]{1,2,0:T(8,128)} custom-call(f32[8,128,128]{2,1,0:T(8,128)S(1)} %get-tuple-element.82), custom_call_target="InvertDiagBlocksLowerTriangular" | custom-call | tf_op jit(solution)/shard_map/jit(_cho_solve)/triangular_solve | solution.py:26
  414.2 11.9 %cholesky.786 = f32[128,128]{1,0:T(8,128)S(1)} custom-call(f32[128,128]{1,0:T(8,128)S(1)} %convolution_subtract_fusion.27), custom_call_target="Cholesky" | custom-call | tf_op jit(solution)/shard_map/jit(cholesky)/cholesky | solution.py:47
  434.4 20.5 %custom-call.110 = f32[2,128,128]{1,2,0:T(8,128)S(1)} custom-call(f32[2,128,128]{2,1,0:T(8,128)} %copy-done.27), custom_call_target="InvertDiagBlocksLowerTriangular" | custom-call | tf_op jit(solution)/shard_map/jit(_cho_solve)/triangular_solve | solution.py:48
  499.0 12.1 %cholesky.803 = f32[128,128]{1,0:T(8,128)S(1)} custom-call(f32[128,128]{1,0:T(8,128)S(1)} %cholesky.943), custom_call_target="Cholesky" | custom-call | tf_op jit(solution)/shard_map/jit(cholesky)/cholesky | solution.py:47
  523.1 11.7 %cholesky.813 = f32[128,128]{1,0:T(8,128)S(1)} custom-call(f32[128,128]{1,0:T(8,128)S(1)} %convolution_subtract_fusion.26), custom_call_target="Cholesky" | custom-call | tf_op jit(solution)/shard_map/jit(cholesky)/cholesky | solution.py:47
  543.2 20.7 %custom-call.111 = f32[2,128,128]{1,2,0:T(8,128)S(1)} custom-call(f32[2,128,128]{2,1,0:T(8,128)} %copy-done.28), custom_call_target="InvertDiagBlocksLowerTriangular" | custom-call | tf_op jit(solution)/shard_map/jit(_cho_solve)/triangular_solve | solution.py:48
  611.3 11.9 %cholesky.830 = f32[128,128]{1,0:T(8,128)S(1)} custom-call(f32[128,128]{1,0:T(8,128)S(1)} %cholesky.946), custom_call_target="Cholesky" | custom-call | tf_op jit(solution)/shard_map/jit(cholesky)/cholesky | solution.py:47
  635.2 11.7 %cholesky.840 = f32[128,128]{1,0:T(8,128)S(1)} custom-call(f32[128,128]{1,0:T(8,128)S(1)} %convolution_subtract_fusion.25), custom_call_target="Cholesky" | custom-call | tf_op jit(solution)/shard_map/jit(cholesky)/cholesky | solution.py:47
  655.1 20.9 %custom-call.112 = f32[2,128,128]{1,2,0:T(8,128)S(1)} custom-call(f32[2,128,128]{2,1,0:T(8,128)} %copy-done.29), custom_call_target="InvertDiagBlocksLowerTriangular" | custom-call | tf_op jit(solution)/shard_map/jit(_cho_solve)/triangular_solve | solution.py:48
  723.2 11.8 %cholesky.857 = f32[128,128]{1,0:T(8,128)S(1)} custom-call(f32[128,128]{1,0:T(8,128)S(1)} %cholesky.949), custom_call_target="Cholesky" | custom-call | tf_op jit(solution)/shard_map/jit(cholesky)/cholesky | solution.py:47
  747.1 11.7 %cholesky.867 = f32[128,128]{1,0:T(8,128)S(1)} custom-call(f32[128,128]{1,0:T(8,128)S(1)} %convolution_subtract_fusion.24), custom_call_target="Cholesky" | custom-call | tf_op jit(solution)/shard_map/jit(cholesky)/cholesky | solution.py:47
  766.9 20.7 %custom-call.113 = f32[2,128,128]{1,2,0:T(8,128)S(1)} custom-call(f32[2,128,128]{2,1,0:T(8,128)} %copy-done.30), custom_call_target="InvertDiagBlocksLowerTriangular" | custom-call | tf_op jit(solution)/shard_map/jit(_cho_solve)/triangular_solve | solution.py:48
  824.5 11.7 %cholesky.884 = f32[128,128]{1,0:T(8,128)S(1)} custom-call(f32[128,128]{1,0:T(8,128)S(1)} %cholesky.952), custom_call_target="Cholesky" | custom-call | tf_op jit(solution)/shard_map/jit(cholesky)/cholesky | solution.py:47
  847.4 13.3 %cholesky.894 = f32[128,128]{1,0:T(8,128)} custom-call(f32[128,128]{1,0:T(8,128)} %convolution_subtract_fusion.23), custom_call_target="Cholesky" | custom-call | tf_op jit(solution)/shard_map/jit(cholesky)/cholesky | solution.py:47
  871.0 21.1 %custom-call.114 = f32[2,128,128]{1,2,0:T(8,128)} custom-call(f32[2,128,128]{2,1,0:T(8,128)} %get-tuple-element.122), custom_call_target="InvertDiagBlocksLowerTriangular" | custom-call | tf_op jit(solution)/shard_map/jit(_cho_solve)/triangular_solve | solution.py:48
  (439 shorter events, 521.5 us)
Async XLA Ops:
  341.1 3.3 copy-start.1
  372.5 2.0 collective-permute-start
  375.6 3.9 copy-start.14
  470.5 1.7 collective-permute-start.1
  472.3 11.1 %collective-permute-start.2 = (f32[128,640]{1,0:T(8,128)S(1)}, f32[128,640]{1,0:T(8,128)}, u32[]{:S(2)}, u32[]{:S(2)}) collective-permute-start(f32[128,640]{1,0:T(8,128)S(1)} %add.328), channel_id=1, source_target_pairs={{0,2},{1,3},{2,0},{3,1},{4,6},{5,7},{6,4},{7,5},{8,10},{9,11},{10,... | collective-permute-start | bytes 983048 | tf_op jit(solution)/shard_map/ppermute | solution.py:14
  484.3 3.8 copy-start.15
  577.9 1.6 collective-permute-start.3
  579.5 8.4 collective-permute-start.4
  588.0 7.7 collective-permute-start.5
  596.7 3.6 copy-start.16
  602.8 2.9 copy-start.11
  688.3 1.5 collective-permute-start.6
  689.8 7.0 collective-permute-start.7
  696.8 6.2 collective-permute-start.8
  703.0 5.7 collective-permute-start.9
  708.8 3.4 copy-start.17
  797.3 24.8 %copy-start = (f32[5,256,256]{2,1,0:T(8,128)S(1)}, f32[5,256,256]{2,1,0:T(8,128)}, u32[]{:S(2)}) copy-start(f32[5,256,256]{2,1,0:T(8,128)} %param.26) | copy-start | bytes 3932164
  797.4 1.3 collective-permute-start.10
  798.7 5.6 collective-permute-start.11
  804.4 5.0 collective-permute-start.12
  809.4 5.0 collective-permute-start.13
  814.5 7.6 collective-permute-start.14
  847.4 50.8 %copy-start.4 = (f32[1024,384]{1,0:T(8,128)S(1)}, f32[1024,384]{1,0:T(8,128)}, u32[]{:S(2)}) copy-start(f32[1024,384]{1,0:T(8,128)} %copy-done.3) | copy-start | bytes 4718596
  892.1 7.1 slice-start
  (23 other events, 38.4 us)
where the time goes:
time: 907 us; the launch traced here: 900 us
  other arithmetic  571 us (63%)
  matrix products  147 us (16%)
  local copies, waits for them, and re-layouts  90.6 us (10%)
  waiting for transfers between devices  55.7 us (6%)
  starting transfers between devices  21.8 us (2%)
  between operations  13.8 us (2%)
    another operation x35, other arithmetic, couple(): lower_tri = jnp.linalg.cholesky(coupled)  177 us
    another operation x30, other arithmetic, leaf_solve(): lower_tri = jnp.linalg.cholesky(kernel)  172 us
    another operation x11, other arithmetic, couple(): solved_coef = jax.scipy.linalg.cho_solve((lower_tri, True), forcing)  109 us
    another operation x3, other arithmetic, leaf_solve(): solved = jax.scipy.linalg.cho_solve((lower_tri, True), stacked)  84.4 us
    ppermute x15, waiting for transfers between devices, swapped(): lax.ppermute(shard, axis, [(i, i ^ 1 << stride) for i in range(lax.axis_s...  55.7 us
    another operation x56, local copies, waits for them, and re-layouts  43.5 us
    another operation x30, matrix products, leaf_solve(): solved = jax.scipy.linalg.cho_solve((lower_tri, True), stacked)  23.6 us
    another operation x14, matrix products, leaf_solve(): lower_tri = jnp.linalg.cholesky(kernel)  23.1 us
  transfers between devices with their start and end apart: 15, of which 15 were waited for; matrix products, arithmetic and copies ran while one was open for 0% of the time, Pallas kernels for 0%

commit v1 on v0

v1 whole, which is shorter than its diff:
```python
import functools
import math

import jax
import jax.numpy as jnp
from jax import lax
from jax.experimental import pallas as pl
from jax.experimental.pallas import tpu as pltpu
from jax.sharding import PartitionSpec as P

R = 128
GAMMA_RATE = 2.0
NUGGET_VALUE = 1.0
HIGH = lax.Precision.HIGH
HIGHEST = lax.Precision.HIGHEST


def nn(a, b, precision=HIGH):
    return lax.dot_general(
        a, b, (((1,), (0,)), ((), ())), precision=precision, preferred_element_type=jnp.float32
    )


def nt(a, b, precision=HIGH):
    return lax.dot_general(
        a, b, (((1,), (1,)), ((), ())), precision=precision, preferred_element_type=jnp.float32
    )


def identity(size):
    row = lax.broadcasted_iota(jnp.int32, (size, size), 0)
    col = lax.broadcasted_iota(jnp.int32, (size, size), 1)
    return (row == col).astype(jnp.float32)


def inverse(matrix, refine):
    size = matrix.shape[0]
    eye = identity(size)
    low = 1.0 / jnp.max(jnp.sum(jnp.abs(matrix), axis=0))

    def step(carry):
        low, x, z = carry
        scale = 4.0 / ((1.0 + low) * (1.0 + low))
        shift = 1.0 + low
        return (
            low * scale,
            scale * (shift * x - nn(x, z)),
            scale * (shift * z - nn(z, z)),
        )

    _, x, _ = lax.while_loop(
        lambda carry: carry[0] < 1.0 - 6e-7, step, (low, eye * low, matrix * low)
    )
    if refine:
        x = x + nn(x, eye - nn(matrix, x, HIGHEST))
    return x


def leaf_kernel(
    count_ref, points_ref, order_ref, basis_ref, rhs_ref,
    head_ref, rest_ref, factor_ref, rows_ref, coords_ref, weighted_ref,
):
    slots = points_ref.shape[1]
    levels = basis_ref.shape[1] // R
    blocks = levels + 1
    tile = min(256, slots)
    count = count_ref[0]
    coords_ref[...] = jnp.zeros_like(coords_ref)
    coords_ref[0:3, :] = points_ref[...]
    coords = coords_ref[...]
    first = coords.astype(jnp.bfloat16).astype(jnp.float32)
    second = (coords - first).astype(jnp.bfloat16).astype(jnp.float32)
    third = coords - first - second
    parts = jnp.concatenate([first, second, third], axis=0).astype(jnp.bfloat16)
    source = lax.broadcasted_iota(jnp.int32, (slots, slots), 0)
    chosen = jnp.where(source == order_ref[...], 1.0, 0.0).astype(jnp.bfloat16)
    moved = jnp.dot(parts, chosen, preferred_element_type=jnp.float32)
    across = moved[0:8] + moved[8:16] + moved[16:24]
    down = across.T
    live_across = (lax.broadcasted_iota(jnp.int32, (1, slots), 1) < count).astype(jnp.float32)
    live_down = (lax.broadcasted_iota(jnp.int32, (slots, 1), 0) < count).astype(jnp.float32)
    for block in range(blocks):
        if block < levels:
            piece = basis_ref[:, block * R : (block + 1) * R]
        else:
            piece = rhs_ref[...]
        rows_ref[block * R : (block + 1) * R, :] = piece.T * live_across
    steps = slots // tile
    for j in range(steps):
        js = slice(j * tile, (j + 1) * tile)
        for i in range(j, steps):
            rs = slice(i * tile, (i + 1) * tile)
            total = None
            for axis in range(3):
                offset = down[rs, axis : axis + 1] - across[axis : axis + 1, js]
                square = offset * offset
                total = square if total is None else total + square
            value = jnp.exp2(total * (-GAMMA_RATE * math.log2(math.e)))
            value = value * live_down[rs] * live_across[:, js]
            if i == j:
                value = value + NUGGET_VALUE * identity(tile)
            factor_ref[rs, js] = value
    for k in range(steps):
        ks = slice(k * tile, (k + 1) * tile)
        x = inverse(factor_ref[ks, ks], False)
        factor_ref[ks, ks] = x
        own = rows_ref[:, ks]
        if k < steps - 1:
            panel = factor_ref[(k + 1) * tile :, ks]
            lower = nn(panel, x)
            factor_ref[(k + 1) * tile :, ks] = lower
            for j in range(k + 1, steps):
                js = slice(j * tile, (j + 1) * tile)
                at = (j - k - 1) * tile
                factor_ref[j * tile :, js] -= nt(lower[at:], panel[at : at + tile])
            rows_ref[:, (k + 1) * tile :] -= nt(own, lower)
        weighted_ref[:, ks] = nn(own, x)
    at = -R
    for m in range(levels):
        column = nt(weighted_ref[m * R :, :], rows_ref[m * R : (m + 1) * R, :])
        if m == 0:
            head_ref[...] = column[:R]
            rest_ref[0 : levels * R, :] = column[R:]
        else:
            rest_ref[at : at + (blocks - m) * R, :] = column
        at += (blocks - m) * R


def packed_rows(levels, level):
    return sum(levels + 1 - m for m in range(level, levels)) * R - R


def invert_kernel(side_ref, own_ref, sibling_ref, factor_ref, inverse_ref):
    side = side_ref[0]
    mine = factor_ref[0, pl.ds(pl.multiple_of(side * R, R), R), :]
    theirs = factor_ref[0, pl.ds(pl.multiple_of((1 - side) * R, R), R), :]
    pair = jnp.concatenate([mine, theirs], axis=0)
    inner = jnp.concatenate([nn(own_ref[...], mine), nn(sibling_ref[...], theirs)], axis=0)
    coupled = identity(2 * R) + nn(pair.T, inner)
    coupled = 0.5 * (coupled + coupled.T)
    inverse_ref[...] = inverse(coupled, True)


def condense_kernel(
    level, levels, side_ref, own_ref, sibling_ref, inverse_ref, factor_ref, gain_ref, *next_refs
):
    side = side_ref[0]
    mine = factor_ref[0, pl.ds(pl.multiple_of(side * R, R), R), :]
    theirs = factor_ref[0, pl.ds(pl.multiple_of((1 - side) * R, R), R), :]
    pair = jnp.concatenate([mine, theirs], axis=0)
    height = (levels - level) * R
    forcing = nn(jnp.concatenate([own_ref[:height], sibling_ref[:height]], axis=1), pair)
    coefficients = nn(forcing, inverse_ref[...])
    if next_refs:
        head_ref, rest_ref = next_refs
        at, to = height, -R
        for m in range(level + 1, levels):
            low = (m - level - 1) * R
            column = own_ref[at : at + height - low] + sibling_ref[at : at + height - low]
            column = column - nt(coefficients[low:], forcing[low : low + R])
            if m == level + 1:
                head_ref[...] = column[:R]
                rest_ref[0 : height - R, :] = column[R:]
            else:
                rest_ref[to : to + height - low, :] = column
            at += height - low
            to += height - low
    gain_ref[...] = nt(coefficients, mine)


def finish_kernel(levels, rows_ref, factor_ref, *refs):
    gain_refs, out_ref, weights_ref = refs[:levels], refs[levels], refs[levels + 1]
    slots = rows_ref.shape[1]
    tile = min(256, slots)
    steps = slots // tile
    for level in reversed(range(levels)):
        gain = gain_refs[level]
        at = (levels - level - 1) * R
        weight = gain[at : at + R]
        if at > 0:
            weight = weight - nn(weights_ref[:, (level + 1) * R :], gain[0:at])
        weights_ref[:, level * R : (level + 1) * R] = weight
    right = rows_ref[levels * R :, :] - nn(weights_ref[...], rows_ref[: levels * R, :])
    solved = [None] * steps
    for k in reversed(range(steps)):
        ks = slice(k * tile, (k + 1) * tile)
        value = nn(right[:, ks], factor_ref[ks, ks])
        if k < steps - 1:
            later = jnp.concatenate(solved[k + 1 :], axis=1)
            value = value - nn(later, factor_ref[(k + 1) * tile :, ks])
        solved[k] = value
    out_ref[...] = jnp.concatenate(solved, axis=1).T


def swapped(shard, axis, stride):
    return lax.ppermute(shard, axis, [(i, i ^ 1 << stride) for i in range(lax.axis_size(axis))])


def pair_swap(payload, bit_index, sub_bits):
    if bit_index < sub_bits:
        return swapped(payload, "sub", bit_index)
    return swapped(payload, "leaf", bit_index - sub_bits)


def f32(*shape):
    return jax.ShapeDtypeStruct(shape, jnp.float32)


VMEM = pl.BlockSpec(memory_space=pltpu.VMEM)
SMEM = pl.BlockSpec(memory_space=pltpu.SMEM)


def shards(points, order, counts, basis, right_side, coupling):
    slots = points.shape[1]
    levels = basis.shape[1] // R
    columns = (levels + 1) * R
    sub_bits = lax.axis_size("sub").bit_length() - 1
    position = lax.axis_index("leaf") * lax.axis_size("sub") + lax.axis_index("sub")
    head, rest, factor, rows = pl.pallas_call(
        leaf_kernel,
        out_shape=(
            f32(R, R), f32(packed_rows(levels, 0), R), f32(slots, slots), f32(columns, slots),
        ),
        in_specs=[SMEM] + [VMEM] * 4,
        out_specs=(VMEM,) * 4,
        scratch_shapes=[pltpu.VMEM((8, slots), jnp.float32), pltpu.VMEM((columns, slots), jnp.float32)],
        name="leaf",
    )(counts, points, order, basis, right_side)
    gains = []
    for level in range(levels):
        side = (position >> level & 1).astype(jnp.int32).reshape(1)
        other_head = pair_swap(head, level, sub_bits)
        other_rest = pair_swap(rest, level, sub_bits)
        chosen = pl.BlockSpec((1, 2 * R, 2 * R), functools.partial(lambda at, i: (at, 0, 0), level))
        whole = lambda *shape: pl.BlockSpec(shape, lambda i: (0, 0))
        inverted = pl.pallas_call(
            invert_kernel,
            grid=(1,),
            out_shape=f32(2 * R, 2 * R),
            in_specs=[SMEM, whole(R, R), whole(R, R), chosen],
            out_specs=whole(2 * R, 2 * R),
            name=f"invert{level}",
        )(side, head, other_head, coupling)
        shapes = [f32((levels - level) * R, R)]
        if level < levels - 1:
            shapes += [f32(R, R), f32(packed_rows(levels, level + 1), R)]
        outs = pl.pallas_call(
            functools.partial(condense_kernel, level, levels),
            grid=(1,),
            out_shape=shapes,
            in_specs=[SMEM, whole(*rest.shape), whole(*rest.shape), whole(2 * R, 2 * R), chosen],
            out_specs=[whole(*s.shape) for s in shapes],
            name=f"condense{level}",
        )(side, rest, other_rest, inverted, coupling)
        gains.append(outs[0])
        if level < levels - 1:
            head, rest = outs[1:]
    return pl.pallas_call(
        functools.partial(finish_kernel, levels),
        out_shape=f32(slots, R),
        in_specs=[VMEM] * (2 + levels),
        out_specs=VMEM,
        scratch_shapes=[pltpu.VMEM((R, levels * R), jnp.float32)],
        name="finish",
    )(rows, factor, *gains)


def solution(mesh):
    placed = (
        P(None, ("leaf", "sub")),
        P(("leaf", "sub"), None),
        P(("leaf", "sub")),
        P(("leaf", "sub"), None),
        P(("leaf", "sub"), None),
        P(),
    )
    return jax.shard_map(
        shards, mesh=mesh, in_specs=placed, out_specs=P(("leaf", "sub"), None), check_vma=False
    )
```

time: 907 us -> 147 us (0.16)
  other arithmetic: 571 us -> 0 us
  matrix products: 147 us -> 0 us
  local copies, waits for them, and re-layouts: 90.6 us -> 7.25 us
  Pallas kernels: 0 us -> 80 us
  between operations: 13.8 us -> 0.68 us
  starting transfers between devices: 21.8 us -> 11.9 us
    another operation x79 -> x0, other arithmetic: 542 us -> none  [the longest x35 177 us: couple(): lower_tri = jnp.linalg.cholesky(coupled)]
    pallas_call x0 -> x12, Pallas kernels: none -> 80 us  [the longest x5 30.7 us: shards(): pl.pallas_call(invert_kernel, grid=(1,), out_shape=f32(2 * R, 2 * R), in_...]
    dot_general x45 -> x0, matrix products: 74.3 us -> none  [the longest x5 16.8 us: shards(): jnp.dot(solved[:, col_start:col_start + R], own_mixed, precision=highest)]
    another operation x84 -> x0, matrix products: 72.8 us -> none  [the longest x30 23.6 us: leaf_solve(): solved = jax.scipy.linalg.cho_solve((lower_tri, True), stacked)]
    another operation x80 -> x0, local copies, waits for them, and re-layouts: 46.3 us -> none
    dot_general x10 -> x0, local copies, waits for them, and re-layouts: 10.7 us -> none  [the longest x5 7.25 us: couple(): jnp.dot(lower_half.T, jnp.dot(second_block, lower_half, precision=highest...]
    ppermute x15 -> x10, starting transfers between devices: 21.8 us -> 11.9 us  [swapped(): lax.ppermute(shard, axis, [(i, i ^ 1 << stride) for i in range(lax.axis_s...]
    ppermute x15 -> x10, waiting for transfers between devices: 55.7 us -> 46.8 us  [swapped(): lax.ppermute(shard, axis, [(i, i ^ 1 << stride) for i in range(lax.axis_s...]
  transfers between devices with their start and end apart: 15 -> 10, of which waited for: 15 -> 5; matrix products, arithmetic and copies ran while one was open for 0% -> 0% of each run, Pallas kernels for 0% -> 21%
where the time goes in v1:
time: 147 us
  Pallas kernels  80 us (54%)
  waiting for transfers between devices  46.8 us (32%)
  starting transfers between devices  11.9 us (8%)
  local copies, waits for them, and re-layouts  7.25 us (5%)
    ppermute x10, waiting for transfers between devices, swapped(): lax.ppermute(shard, axis, [(i, i ^ 1 << stride) for i in range(lax.axis_s...  46.8 us
    pallas_call x5, Pallas kernels, shards(): pl.pallas_call(invert_kernel, grid=(1,), out_shape=f32(2 * R, 2 * R), in_...  30.7 us
    pallas_call x1, Pallas kernels, shards(): pl.pallas_call(leaf_kernel, out_shape=(f32(R, R), f32(packed_rows(levels,...  25.5 us
    pallas_call x5, Pallas kernels, shards(): pl.pallas_call(functools.partial(condense_kernel, level, levels), grid=(1...  16.9 us
    ppermute x10, starting transfers between devices, swapped(): lax.ppermute(shard, axis, [(i, i ^ 1 << stride) for i in range(lax.axis_s...  11.9 us
    unnamed x20, local copies, waits for them, and re-layouts  7.25 us
    pallas_call x1, Pallas kernels, shards(): pl.pallas_call(functools.partial(finish_kernel, levels), out_shape=f32(sl...  6.88 us
  transfers between devices with their start and end apart: 10, of which 5 were waited for; matrix products, arithmetic and copies ran while one was open for 0% of the time, Pallas kernels for 21%

profile of v1, /device:TPU:0, one launch (start us, length us, event | category | flops | bytes accessed | tf_op | source)
XLA Modules:
  0.0 146.7 jit_solution(14752602771383929795)
XLA Ops:
  0.7 25.5 %leaf.1 = (f32[128,128]{1,0:T(8,128)}, f32[2432,128]{1,0:T(8,128)}, f32[1024,1024]{1,0:T(8,128)}, f32[768,1024]{1,0:T(8,128)}) custom-call(s32[1]{0:T(128)S(6)} %copy.7.count_ref, f32[3,1024]{1,0:T(4,128)} %points_ref.1, s32[1,1024]{1,0:T(1,128)} %order_ref.1, f32[1024,640]{1,0:T(8,128)} %basis_ref.1, f32[1024,128]{1,0:T(8,128)} %rhs_ref.1), custom_call_target="tpu_custom_call" | custom-call | tf_op jit(solution)/shard_map/leaf/pallas_call | solution.py:219
  26.7 2.7 %collective-permute-done.1.sibling_ref = f32[128,128]{1,0:T(8,128)S(1)} collective-permute-done((f32[128,128]{1,0:T(8,128)}, f32[128,128]{1,0:T(8,128)S(1)}, u32[]{:S(2)}, u32[]{:S(2)}) %collective-permute-start.1) | collective-permute-done | bytes 65568 | tf_op jit(solution)/shard_map/ppermute | solution.py:196
  30.1 5.7 %invert0.1.inverse_ref = f32[256,256]{1,0:T(8,128)} custom-call(s32[1]{0:T(128)} %bitcast.side_ref, f32[128,128]{1,0:T(8,128)} %get-tuple-element.24.own_ref, f32[128,128]{1,0:T(8,128)} %copy-done.4, f32[5,256,256]{2,1,0:T(8,128)} %factor_ref.19), custom_call_target="tpu_custom_call" | custom-call | tf_op jit(solution)/shard_map/invert0/pallas_call | solution.py:236
  35.7 1.1 copy-done
  36.8 4.6 %condense0.1 = (f32[640,128]{1,0:T(8,128)}, f32[128,128]{1,0:T(8,128)}, f32[1664,128]{1,0:T(8,128)}) custom-call(s32[1]{0:T(128)} %bitcast.side_ref, f32[2432,128]{1,0:T(8,128)} %get-tuple-element.23.own_ref, f32[2432,128]{1,0:T(8,128)} %copy-done, f32[256,256]{1,0:T(8,128)} %invert0.1.inverse_ref, f32[5,256,256]{2,1,0:T(8,128)} %factor_ref.19), custom_call_target="tpu_custom_call" | custom-call | tf_op jit(solution)/shard_map/condense0/pallas_call | solution.py:247
  41.4 1.0 collective-permute-start.2
  42.4 1.0 collective-permute-start.3
  43.4 20.6 %collective-permute-done.3.sibling_ref = f32[128,128]{1,0:T(8,128)S(1)} collective-permute-done((f32[128,128]{1,0:T(8,128)}, f32[128,128]{1,0:T(8,128)S(1)}, u32[]{:S(2)}, u32[]{:S(2)}) %collective-permute-start.3) | collective-permute-done | bytes 65568 | tf_op jit(solution)/shard_map/ppermute | solution.py:196
  64.6 5.9 %invert1.1.inverse_ref = f32[256,256]{1,0:T(8,128)} custom-call(s32[1]{0:T(128)} %bitcast.1.side_ref, f32[128,128]{1,0:T(8,128)} %get-tuple-element.27.own_ref, f32[128,128]{1,0:T(8,128)} %copy-done.8, f32[5,256,256]{2,1,0:T(8,128)} %factor_ref.19), custom_call_target="tpu_custom_call" | custom-call | tf_op jit(solution)/shard_map/invert1/pallas_call | solution.py:236
  70.5 1.0 copy-done.1
  71.5 3.9 %condense1.1 = (f32[512,128]{1,0:T(8,128)}, f32[128,128]{1,0:T(8,128)}, f32[1024,128]{1,0:T(8,128)}) custom-call(s32[1]{0:T(128)} %bitcast.1.side_ref, f32[1664,128]{1,0:T(8,128)} %get-tuple-element.26.own_ref, f32[1664,128]{1,0:T(8,128)} %copy-done.1, f32[256,256]{1,0:T(8,128)} %invert1.1.inverse_ref, f32[5,256,256]{2,1,0:T(8,128)} %factor_ref.19), custom_call_target="tpu_custom_call" | custom-call | tf_op jit(solution)/shard_map/condense1/pallas_call | solution.py:247
  75.3 4.0 %collective-permute-start.4 = (f32[1024,128]{1,0:T(8,128)}, f32[1024,128]{1,0:T(8,128)S(1)}, u32[]{:S(2)}, u32[]{:S(2)}) collective-permute-start(f32[1024,128]{1,0:T(8,128)} %get-tuple-element.29.own_ref), channel_id=1, source_target_pairs={{0,4},{4,0},{8,12},{12,8},{16,20},{20,16},{24,28},{28,24},{1,5},{5... | collective-permute-start | bytes 1572872 | tf_op jit(solution)/shard_map/ppermute | solution.py:196
  79.4 13.1 %collective-permute-done.5.sibling_ref = f32[128,128]{1,0:T(8,128)S(1)} collective-permute-done((f32[128,128]{1,0:T(8,128)}, f32[128,128]{1,0:T(8,128)S(1)}, u32[]{:S(2)}, u32[]{:S(2)}) %collective-permute-start.5) | collective-permute-done | bytes 65568 | tf_op jit(solution)/shard_map/ppermute | solution.py:196
  93.1 6.1 %invert2.1.inverse_ref = f32[256,256]{1,0:T(8,128)} custom-call(s32[1]{0:T(128)} %bitcast.2.side_ref, f32[128,128]{1,0:T(8,128)} %get-tuple-element.30.own_ref, f32[128,128]{1,0:T(8,128)} %copy-done.6, f32[5,256,256]{2,1,0:T(8,128)} %factor_ref.19), custom_call_target="tpu_custom_call" | custom-call | tf_op jit(solution)/shard_map/invert2/pallas_call | solution.py:236
  100.0 3.3 %condense2.1 = (f32[384,128]{1,0:T(8,128)}, f32[128,128]{1,0:T(8,128)}, f32[512,128]{1,0:T(8,128)}) custom-call(s32[1]{0:T(128)} %bitcast.2.side_ref, f32[1024,128]{1,0:T(8,128)} %get-tuple-element.29.own_ref, f32[1024,128]{1,0:T(8,128)} %copy-done.2, f32[256,256]{1,0:T(8,128)} %invert2.1.inverse_ref, f32[5,256,256]{2,1,0:T(8,128)} %factor_ref.19), custom_call_target="tpu_custom_call" | custom-call | tf_op jit(solution)/shard_map/condense2/pallas_call | solution.py:247
  103.3 2.4 %collective-permute-start.6 = (f32[512,128]{1,0:T(8,128)}, f32[512,128]{1,0:T(8,128)S(1)}, u32[]{:S(2)}, u32[]{:S(2)}) collective-permute-start(f32[512,128]{1,0:T(8,128)} %get-tuple-element.32.own_ref), channel_id=1, source_target_pairs={{0,8},{4,12},{8,0},{12,4},{16,24},{20,28},{24,16},{28,20},{1,9},{5... | collective-permute-start | bytes 786440 | tf_op jit(solution)/shard_map/ppermute | solution.py:196
  105.8 6.5 %collective-permute-done.7.sibling_ref = f32[128,128]{1,0:T(8,128)S(1)} collective-permute-done((f32[128,128]{1,0:T(8,128)}, f32[128,128]{1,0:T(8,128)S(1)}, u32[]{:S(2)}, u32[]{:S(2)}) %collective-permute-start.7) | collective-permute-done | bytes 65568 | tf_op jit(solution)/shard_map/ppermute | solution.py:196
  112.9 6.5 %invert3.1.inverse_ref = f32[256,256]{1,0:T(8,128)} custom-call(s32[1]{0:T(128)} %bitcast.3.side_ref, f32[128,128]{1,0:T(8,128)} %get-tuple-element.33.own_ref, f32[128,128]{1,0:T(8,128)} %copy-done.7, f32[5,256,256]{2,1,0:T(8,128)} %factor_ref.19), custom_call_target="tpu_custom_call" | custom-call | tf_op jit(solution)/shard_map/invert3/pallas_call | solution.py:236
  120.1 2.8 %condense3.1 = (f32[256,128]{1,0:T(8,128)}, f32[128,128]{1,0:T(8,128)}, f32[128,128]{1,0:T(8,128)}) custom-call(s32[1]{0:T(128)} %bitcast.3.side_ref, f32[512,128]{1,0:T(8,128)} %get-tuple-element.32.own_ref, f32[512,128]{1,0:T(8,128)} %copy-done.3, f32[256,256]{1,0:T(8,128)} %invert3.1.inverse_ref, f32[5,256,256]{2,1,0:T(8,128)} %factor_ref.19), custom_call_target="tpu_custom_call" | custom-call | tf_op jit(solution)/shard_map/condense3/pallas_call | solution.py:247
  122.9 2.3 %collective-permute-start.9 = (f32[128,128]{1,0:T(8,128)}, f32[128,128]{1,0:T(8,128)S(1)}, u32[]{:S(2)}, u32[]{:S(2)}) collective-permute-start(f32[128,128]{1,0:T(8,128)} %get-tuple-element.36.own_ref), channel_id=1, source_target_pairs={{0,16},{4,20},{8,24},{12,28},{16,0},{20,4},{24,8},{28,12},{1,17},{... | collective-permute-start | bytes 196616 | tf_op jit(solution)/shard_map/ppermute | solution.py:196
  125.8 3.9 %collective-permute-done.9.sibling_ref = f32[128,128]{1,0:T(8,128)S(1)} collective-permute-done((f32[128,128]{1,0:T(8,128)}, f32[128,128]{1,0:T(8,128)S(1)}, u32[]{:S(2)}, u32[]{:S(2)}) %collective-permute-start.9) | collective-permute-done | bytes 65568 | tf_op jit(solution)/shard_map/ppermute | solution.py:196
  130.3 6.5 %invert4.1.inverse_ref = f32[256,256]{1,0:T(8,128)} custom-call(s32[1]{0:T(128)} %bitcast.4.side_ref, f32[128,128]{1,0:T(8,128)} %get-tuple-element.36.own_ref, f32[128,128]{1,0:T(8,128)} %copy-done.5, f32[5,256,256]{2,1,0:T(8,128)} %factor_ref.19), custom_call_target="tpu_custom_call" | custom-call | tf_op jit(solution)/shard_map/invert4/pallas_call | solution.py:236
  137.5 2.3 %condense4.1.refs_4_ = f32[128,128]{1,0:T(8,128)} custom-call(s32[1]{0:T(128)} %bitcast.4.side_ref, f32[128,128]{1,0:T(8,128)} %get-tuple-element.35.own_ref, f32[128,128]{1,0:T(8,128)} %copy-done.9, f32[256,256]{1,0:T(8,128)} %invert4.1.inverse_ref, f32[5,256,256]{2,1,0:T(8,128)} %factor_ref.19), custom_call_target="tpu_custom_call" | custom-call | tf_op jit(solution)/shard_map/condense4/pallas_call | solution.py:247
  139.8 6.9 %finish.1 = f32[1024,128]{1,0:T(8,128)} custom-call(f32[768,1024]{1,0:T(8,128)} %get-tuple-element.21.rows_ref, f32[1024,1024]{1,0:T(8,128)} %get-tuple-element.22.factor_ref, f32[640,128]{1,0:T(8,128)} %get-tuple-element.25.refs_0_, f32[512,128]{1,0:T(8,128)} %get-tuple-element.28.refs_1_, f32[384,128]{1,0:T(8,128)} %get-tuple-element.31.refs_2_, ...), custom_call_target="tpu_custom_call" | custom-call | tf_op jit(solution)/shard_map/finish/pallas_call | solution.py:258
  (28 shorter events, 6.4 us)
Async XLA Ops:
  26.2 9.5 %collective-permute-start = (f32[2432,128]{1,0:T(8,128)}, f32[2432,128]{1,0:T(8,128)S(1)}, u32[]{:S(2)}, u32[]{:S(2)}) collective-permute-start(f32[2432,128]{1,0:T(8,128)} %get-tuple-element.23.own_ref), channel_id=1, source_target_pairs={{0,1},{1,0},{2,3},{3,2},{4,5},{5,4},{6,7},{7,6},{8,9},{9,8},{10,11... | collective-permute-start | bytes 3735560 | tf_op jit(solution)/shard_map/ppermute | solution.py:196
  26.2 3.2 %collective-permute-start.1 = (f32[128,128]{1,0:T(8,128)}, f32[128,128]{1,0:T(8,128)S(1)}, u32[]{:S(2)}, u32[]{:S(2)}) collective-permute-start(f32[128,128]{1,0:T(8,128)} %get-tuple-element.24.own_ref), channel_id=1, source_target_pairs={{0,1},{1,0},{2,3},{3,2},{4,5},{5,4},{6,7},{7,6},{8,9},{9,8},{10,11... | collective-permute-start | bytes 196616 | tf_op jit(solution)/shard_map/ppermute | solution.py:196
  29.4 0.6 copy-start.4
  35.7 1.1 copy-start
  41.4 29.1 %collective-permute-start.2 = (f32[1664,128]{1,0:T(8,128)}, f32[1664,128]{1,0:T(8,128)S(1)}, u32[]{:S(2)}, u32[]{:S(2)}) collective-permute-start(f32[1664,128]{1,0:T(8,128)} %get-tuple-element.26.own_ref), channel_id=1, source_target_pairs={{0,2},{1,3},{2,0},{3,1},{4,6},{5,7},{6,4},{7,5},{8,10},{9,11},{10,... | collective-permute-start | bytes 2555912 | tf_op jit(solution)/shard_map/ppermute | solution.py:196
  42.4 21.6 %collective-permute-start.3 = (f32[128,128]{1,0:T(8,128)}, f32[128,128]{1,0:T(8,128)S(1)}, u32[]{:S(2)}, u32[]{:S(2)}) collective-permute-start(f32[128,128]{1,0:T(8,128)} %get-tuple-element.27.own_ref), channel_id=1, source_target_pairs={{0,2},{1,3},{2,0},{3,1},{4,6},{5,7},{6,4},{7,5},{8,10},{9,11},{10,... | collective-permute-start | bytes 196616 | tf_op jit(solution)/shard_map/ppermute | solution.py:196
  64.0 0.6 copy-start.8
  70.5 1.0 copy-start.1
  75.3 23.9 %collective-permute-start.4 = (f32[1024,128]{1,0:T(8,128)}, f32[1024,128]{1,0:T(8,128)S(1)}, u32[]{:S(2)}, u32[]{:S(2)}) collective-permute-start(f32[1024,128]{1,0:T(8,128)} %get-tuple-element.29.own_ref), channel_id=1, source_target_pairs={{0,4},{4,0},{8,12},{12,8},{16,20},{20,16},{24,28},{28,24},{1,5},{5... | collective-permute-start | bytes 1572872 | tf_op jit(solution)/shard_map/ppermute | solution.py:196
  79.4 13.1 %collective-permute-start.5 = (f32[128,128]{1,0:T(8,128)}, f32[128,128]{1,0:T(8,128)S(1)}, u32[]{:S(2)}, u32[]{:S(2)}) collective-permute-start(f32[128,128]{1,0:T(8,128)} %get-tuple-element.30.own_ref), channel_id=1, source_target_pairs={{0,4},{4,0},{8,12},{12,8},{16,20},{20,16},{24,28},{28,24},{1,5},{5... | collective-permute-start | bytes 196616 | tf_op jit(solution)/shard_map/ppermute | solution.py:196
  92.5 0.6 copy-start.6
  99.2 0.8 copy-start.2
  103.3 16.1 %collective-permute-start.6 = (f32[512,128]{1,0:T(8,128)}, f32[512,128]{1,0:T(8,128)S(1)}, u32[]{:S(2)}, u32[]{:S(2)}) collective-permute-start(f32[512,128]{1,0:T(8,128)} %get-tuple-element.32.own_ref), channel_id=1, source_target_pairs={{0,8},{4,12},{8,0},{12,4},{16,24},{20,28},{24,16},{28,20},{1,9},{5... | collective-permute-start | bytes 786440 | tf_op jit(solution)/shard_map/ppermute | solution.py:196
  105.7 6.5 %collective-permute-start.7 = (f32[128,128]{1,0:T(8,128)}, f32[128,128]{1,0:T(8,128)S(1)}, u32[]{:S(2)}, u32[]{:S(2)}) collective-permute-start(f32[128,128]{1,0:T(8,128)} %get-tuple-element.33.own_ref), channel_id=1, source_target_pairs={{0,8},{4,12},{8,0},{12,4},{16,24},{20,28},{24,16},{28,20},{1,9},{5... | collective-permute-start | bytes 196616 | tf_op jit(solution)/shard_map/ppermute | solution.py:196
  112.2 0.6 copy-start.7
  119.4 0.7 copy-start.3
  122.9 6.8 %collective-permute-start.9 = (f32[128,128]{1,0:T(8,128)}, f32[128,128]{1,0:T(8,128)S(1)}, u32[]{:S(2)}, u32[]{:S(2)}) collective-permute-start(f32[128,128]{1,0:T(8,128)} %get-tuple-element.36.own_ref), channel_id=1, source_target_pairs={{0,16},{4,20},{8,24},{12,28},{16,0},{20,4},{24,8},{28,12},{1,17},{... | collective-permute-start | bytes 196616 | tf_op jit(solution)/shard_map/ppermute | solution.py:196
  125.2 11.6 %collective-permute-start.8 = (f32[128,128]{1,0:T(8,128)}, f32[128,128]{1,0:T(8,128)S(1)}, u32[]{:S(2)}, u32[]{:S(2)}) collective-permute-start(f32[128,128]{1,0:T(8,128)} %get-tuple-element.35.own_ref), channel_id=1, source_target_pairs={{0,16},{4,20},{8,24},{12,28},{16,0},{20,4},{24,8},{28,12},{1,17},{... | collective-permute-start | bytes 196616 | tf_op jit(solution)/shard_map/ppermute | solution.py:196
  129.7 0.6 copy-start.5
  136.8 0.6 copy-start.9

commit v2 on v1

v2 whole, which is shorter than its diff:
```python
import functools
import math

import jax
import jax.numpy as jnp
from jax import lax
from jax.experimental import pallas as pl
from jax.experimental.pallas import tpu as pltpu
from jax.sharding import PartitionSpec as P


R = 128
GAMMA_RATE = 2.0
NUGGET_VALUE = 1.0
HIGH = lax.Precision.HIGH
HIGHEST = lax.Precision.HIGHEST


def nn(a, b, precision=HIGH):
    return lax.dot_general(
        a, b, (((1,), (0,)), ((), ())), precision=precision, preferred_element_type=jnp.float32
    )


def nt(a, b, precision=HIGH):
    return lax.dot_general(
        a, b, (((1,), (1,)), ((), ())), precision=precision, preferred_element_type=jnp.float32
    )


def identity(size):
    row = lax.broadcasted_iota(jnp.int32, (size, size), 0)
    col = lax.broadcasted_iota(jnp.int32, (size, size), 1)
    return (row == col).astype(jnp.float32)


def inverse(matrix, refine):
    size = matrix.shape[0]
    eye = identity(size)
    low = 1.0 / jnp.max(jnp.sum(jnp.abs(matrix), axis=0))

    def step(carry):
        low, x, z = carry
        scale = 4.0 / ((1.0 + low) * (1.0 + low))
        shift = 1.0 + low
        return (
            low * scale,
            scale * (shift * x - nn(x, z)),
            scale * (shift * z - nn(z, z)),
        )

    _, x, _ = lax.while_loop(
        lambda carry: carry[0] < 1.0 - 6e-7, step, (low, eye * low, matrix * low)
    )
    if refine:
        x = x + nn(x, eye - nn(matrix, x, HIGHEST))
    return x


def leaf_kernel(
    count_ref, points_ref, order_ref, basis_ref, rhs_ref,
    head_ref, near_rows_ref, far_rows_ref, factor_ref, rows_ref,
    near_points_ref, near_order_ref, coords_ref, weighted_ref, near_basis_ref, near_rhs_ref, sems,
):
    fetches = [
        pltpu.make_async_copy(points_ref, near_points_ref, sems.at[0]),
        pltpu.make_async_copy(order_ref, near_order_ref, sems.at[1]),
        pltpu.make_async_copy(basis_ref, near_basis_ref, sems.at[2]),
        pltpu.make_async_copy(rhs_ref, near_rhs_ref, sems.at[3]),
    ]
    for fetch in fetches:
        fetch.start()
    slots = points_ref.shape[1]
    levels = basis_ref.shape[1] // R
    blocks = levels + 1
    tile = min(256, slots)
    count = count_ref[0]
    coords_ref[...] = jnp.zeros_like(coords_ref)
    fetches[0].wait()
    coords_ref[0:3, :] = near_points_ref[...]
    coords = coords_ref[...]
    first = coords.astype(jnp.bfloat16).astype(jnp.float32)
    second = (coords - first).astype(jnp.bfloat16).astype(jnp.float32)
    third = coords - first - second
    parts = jnp.concatenate([first, second, third], axis=0).astype(jnp.bfloat16)
    source = lax.broadcasted_iota(jnp.int32, (slots, slots), 0)
    fetches[1].wait()
    chosen = jnp.where(source == near_order_ref[...], 1.0, 0.0).astype(jnp.bfloat16)
    moved = jnp.dot(parts, chosen, preferred_element_type=jnp.float32)
    across = moved[0:8] + moved[8:16] + moved[16:24]
    down = across.T
    live_across = (lax.broadcasted_iota(jnp.int32, (1, slots), 1) < count).astype(jnp.float32)
    live_down = (lax.broadcasted_iota(jnp.int32, (slots, 1), 0) < count).astype(jnp.float32)
    steps = slots // tile
    for j in range(steps):
        js = slice(j * tile, (j + 1) * tile)
        for i in range(j, steps):
            rs = slice(i * tile, (i + 1) * tile)
            total = None
            for axis in range(3):
                offset = down[rs, axis : axis + 1] - across[axis : axis + 1, js]
                square = offset * offset
                total = square if total is None else total + square
            value = jnp.exp2(total * (-GAMMA_RATE * math.log2(math.e)))
            value = value * live_down[rs] * live_across[:, js]
            if i == j:
                value = value + NUGGET_VALUE * identity(tile)
            factor_ref[rs, js] = value
    for fetch in fetches[2:]:
        fetch.wait()
    for block in range(blocks):
        if block < levels:
            piece = near_basis_ref[:, block * R : (block + 1) * R]
        else:
            piece = near_rhs_ref[...]
        rows_ref[block * R : (block + 1) * R, :] = piece.T * live_across
    for k in range(steps):
        ks = slice(k * tile, (k + 1) * tile)
        x = inverse(factor_ref[ks, ks], False)
        factor_ref[ks, ks] = x
        own = rows_ref[:, ks]
        if k < steps - 1:
            panel = factor_ref[(k + 1) * tile :, ks]
            lower = nn(panel, x)
            factor_ref[(k + 1) * tile :, ks] = lower
            for j in range(k + 1, steps):
                js = slice(j * tile, (j + 1) * tile)
                at = (j - k - 1) * tile
                factor_ref[j * tile :, js] -= nt(lower[at:], panel[at : at + tile])
            rows_ref[:, (k + 1) * tile :] -= nt(own, lower)
        weighted_ref[:, ks] = nn(own, x)
    for m in range(levels):
        column = nt(weighted_ref[m * R :, :], rows_ref[m * R : (m + 1) * R, :])
        if m == 0:
            head_ref[...] = column[:R]
        for c in range(max(m, 1), blocks):
            piece = column[(c - m) * R : (c - m + 1) * R]
            if c == 1:
                near_rows_ref[:, m * R : (m + 1) * R] = piece
            else:
                at = (row_start(levels, 0, 2, c) + m) * R
                far_rows_ref[:, at : at + R] = piece


def row_blocks(levels, level, row):
    return min(row, levels - 1) - level + 1


def row_start(levels, level, first, row):
    return sum(row_blocks(levels, level, c) for c in range(first, row))


def side_of(level):
    sub_bits = lax.axis_size("sub").bit_length() - 1
    if level < sub_bits:
        return lax.axis_index("sub") >> level & 1
    return lax.axis_index("leaf") >> (level - sub_bits) & 1


def invert_kernel(level, own_ref, sibling_ref, factor_ref, after_ref, inverse_ref, token_ref):
    side = side_of(level)
    mine = factor_ref[level, pl.ds(pl.multiple_of(side * R, R), R), :]
    theirs = factor_ref[level, pl.ds(pl.multiple_of((1 - side) * R, R), R), :]
    pair = jnp.concatenate([mine, theirs], axis=0)
    inner = jnp.concatenate([nn(own_ref[...], mine), nn(sibling_ref[...], theirs)], axis=0)
    coupled = identity(2 * R) + nn(pair.T, inner)
    coupled = 0.5 * (coupled + coupled.T)
    inverse_ref[...] = inverse(coupled, True)
    token_ref[...] = jnp.zeros_like(token_ref)


def condense_kernel(level, levels, group, *refs):
    own_ref, sibling_ref, inverse_ref, factor_ref = refs[:4]
    known = group[0] - level - 1
    forcing_refs, refs = refs[4 : 4 + known], refs[4 + known :]
    refs = refs[1:]
    passed = [row for row in group if row > level + 1 or level < levels - 1]
    next_refs, refs = refs[: len(passed)], refs[len(passed) :]
    new_forcing_refs, gain_refs, token_ref = refs[: len(group)], refs[len(group) : -1], refs[-1]
    side = side_of(level)
    mine = factor_ref[level, pl.ds(pl.multiple_of(side * R, R), R), :]
    theirs = factor_ref[level, pl.ds(pl.multiple_of((1 - side) * R, R), R), :]
    pair = jnp.concatenate([mine, theirs], axis=0)
    starts = [row_start(levels, level, group[0], row) * R for row in group]
    own_side = jnp.concatenate([own_ref[:, at : at + R] for at in starts], axis=0)
    other_side = jnp.concatenate([sibling_ref[:, at : at + R] for at in starts], axis=0)
    forcing = nn(jnp.concatenate([own_side, other_side], axis=1), pair)
    coefficients = nn(forcing, inverse_ref[...])
    gains = nt(coefficients, mine)
    every = [ref[...] for ref in forcing_refs]
    for index, row in enumerate(group):
        piece = forcing[index * R : (index + 1) * R]
        new_forcing_refs[index][...] = piece
        gain_refs[index][...] = gains[index * R : (index + 1) * R]
        every.append(piece)
    for index, row in enumerate(group):
        width = (row_blocks(levels, level, row) - 1) * R
        if width == 0:
            continue
        at = starts[index] + R
        total = own_ref[:, at : at + width] + sibling_ref[:, at : at + width]
        against = jnp.concatenate(every[: width // R], axis=0)
        part = coefficients[index * R : (index + 1) * R]
        next_refs[index][...] = total - nt(part, against)
    token_ref[...] = jnp.zeros_like(token_ref)


def finish_kernel(levels, rows_ref, factor_ref, *refs):
    out_ref, weights_ref = refs[-2:]
    slots = rows_ref.shape[1]
    tile = min(256, slots)
    steps = slots // tile
    end = len(refs) - 2
    for level in reversed(range(levels)):
        start = end - (levels - level)
        weight = refs[end - 1][...]
        if level < levels - 1:
            gain = jnp.concatenate([ref[...] for ref in refs[start : end - 1]], axis=0)
            weight = weight - nn(weights_ref[:, (level + 1) * R :], gain)
        weights_ref[:, level * R : (level + 1) * R] = weight
        end = start
    right = rows_ref[levels * R :, :] - nn(weights_ref[...], rows_ref[: levels * R, :])
    solved = [None] * steps
    for k in reversed(range(steps)):
        ks = slice(k * tile, (k + 1) * tile)
        value = nn(right[:, ks], factor_ref[ks, ks])
        if k < steps - 1:
            later = jnp.concatenate(solved[k + 1 :], axis=1)
            value = value - nn(later, factor_ref[(k + 1) * tile :, ks])
        solved[k] = value
    out_ref[...] = jnp.concatenate(solved, axis=1).T


def swapped(shard, axis, stride):
    return lax.ppermute(shard, axis, [(i, i ^ 1 << stride) for i in range(lax.axis_size(axis))])


def pair_swap(payload, bit_index, sub_bits):
    if bit_index < sub_bits:
        return swapped(payload, "sub", bit_index)
    return swapped(payload, "leaf", bit_index - sub_bits)


def f32(*shape):
    return jax.ShapeDtypeStruct(shape, jnp.float32)


def near(*shape):
    return pltpu.VMEM(shape, jnp.float32)


def far_away(value):
    return pltpu.with_memory_space_constraint(value, pltpu.HBM)


def hold(value):
    return pltpu.with_memory_space_constraint(value, pltpu.VMEM)


VMEM = pl.BlockSpec(memory_space=pltpu.VMEM)
HBM = pl.BlockSpec(memory_space=pltpu.HBM)
SMEM = pl.BlockSpec(memory_space=pltpu.SMEM)
LIMIT = pltpu.CompilerParams(vmem_limit_bytes=12 << 20)
LEAF_LIMIT = pltpu.CompilerParams(vmem_limit_bytes=24 << 20)


def schedule(levels):
    others = tuple(range(2, levels + 1))
    plan = [("invert", 0), ("condense", 0, (1,)), ("condense", 0, others)]
    for level in range(1, levels):
        plan += [("invert", level), ("condense", level, (level + 1,))]
        for at in range(1, level + 1):
            if at > 1 and level + 3 <= levels:
                plan.append(("condense", at - 1, (level + 3,)))
            if level + 2 <= levels:
                plan.append(("condense", at, (level + 2,)))
    return list(dict.fromkeys(plan))


def shards(points, order, counts, basis, right_side, coupling):
    slots = points.shape[1]
    levels = basis.shape[1] // R
    columns = (levels + 1) * R
    sub_bits = lax.axis_size("sub").bit_length() - 1
    coupling = hold(coupling)
    token = near(8, R)
    head, close, far, factor, rows = pl.pallas_call(
        leaf_kernel,
        out_shape=(
            near(R, R), near(R, 2 * R), near(R, row_start(levels, 0, 2, levels + 1) * R),
            near(slots, slots), near(columns, slots),
        ),
        in_specs=[SMEM] + [HBM] * 4,
        out_specs=(VMEM,) * 5,
        scratch_shapes=[
            near(*points.shape), pltpu.VMEM(order.shape, jnp.int32), near(8, slots),
            near(columns, slots), near(*basis.shape), near(*right_side.shape),
            pltpu.SemaphoreType.DMA((4,)),
        ],
        compiler_params=LEAF_LIMIT,
        name="leaf",
    )(counts, *[far_away(x) for x in (points, order, basis, right_side)])

    gains = {}
    forcing = {}
    sent = {}
    inverted = {}
    chain = [jnp.zeros((8, R), jnp.float32)]

    def send(level, group, value):
        sent[level, group] = (value, hold(pair_swap(value, level, sub_bits)))

    def invert(level):
        inverted[level], chain[0] = pl.pallas_call(
            functools.partial(invert_kernel, level),
            out_shape=(near(2 * R, 2 * R), token),
            in_specs=[VMEM] * 4,
            out_specs=[VMEM] * 2,
            compiler_params=LIMIT,
        )(*sent[level, (level,)], coupling, hold(chain[0]))

    def condense(level, group):
        known = range(level + 1, group[0])
        widths = [row_blocks(levels, level, row) - 1 for row in group]
        shapes = [near(R, width * R) for width in widths if width > 0]
        passed = len(shapes)
        shapes += [near(R, 2 * R)] * len(group) + [near(R, R)] * len(group) + [token]
        outs = pl.pallas_call(
            functools.partial(condense_kernel, level, levels, group),
            out_shape=shapes,
            in_specs=[VMEM] * (5 + len(known)),
            out_specs=[VMEM] * len(shapes),
            compiler_params=LIMIT,
        )(
            *sent[level, group], inverted[level], coupling,
            *[forcing[level, row] for row in known], hold(chain[0]),
        )
        chain[0] = outs[-1]
        for index, row in enumerate(group):
            forcing[level, row] = outs[passed + index]
            gains[level, row] = outs[passed + len(group) + index]
        return [(level + 1, (group[index],), outs[index]) for index in range(passed)]

    others = tuple(range(2, levels + 1))
    send(0, (0,), head)
    send(0, (1,), close)
    send(0, others, far)
    for step in schedule(levels):
        if step[0] == "invert":
            invert(step[1])
        else:
            made = condense(*step[1:])
        if step[0] == "condense":
            for one in made:
                send(*one)
    return pl.pallas_call(
        functools.partial(finish_kernel, levels),
        out_shape=f32(slots, R),
        in_specs=[VMEM] * (2 + len(gains)),
        out_specs=VMEM,
        scratch_shapes=[pltpu.VMEM((R, levels * R), jnp.float32)],
        compiler_params=LIMIT,
        name="finish",
    )(rows, factor, *[gains[key] for key in sorted(gains)])


def solution(mesh):
    placed = (
        P(None, ("leaf", "sub")),
        P(("leaf", "sub"), None),
        P(("leaf", "sub")),
        P(("leaf", "sub"), None),
        P(("leaf", "sub"), None),
        P(),
    )

    def step(points, order, counts, basis, right_side, coupling):
        whole = jax.shard_map(
            shards, mesh=mesh, in_specs=placed, out_specs=P(("leaf", "sub"), None), check_vma=False
        )
        return whole(points, order, counts, basis, right_side, coupling)

    return step
```

time: 147 us -> 111 us (0.76)
  Pallas kernels: 80 us -> 60.1 us
  waiting for transfers between devices: 46.8 us -> 28.9 us
  starting transfers between devices: 11.9 us -> 20.5 us
  local copies, waits for them, and re-layouts: 7.25 us -> 0.01 us
    ppermute x10 -> x17, waiting for transfers between devices: 46.8 us -> 28.9 us  [swapped(): lax.ppermute(shard, axis, [(i, i ^ 1 << stride) for i in range(lax.axis_s...]
    pallas_call x11 -> x18, Pallas kernels: 73.1 us -> 56.5 us  [the longest x1 22.9 us: shards(): pl.pallas_call(leaf_kernel, out_shape=(near(R, R), near(R, 2 * R), near(R...]
    ppermute x10 -> x17, starting transfers between devices: 11.9 us -> 20.5 us  [swapped(): lax.ppermute(shard, axis, [(i, i ^ 1 << stride) for i in range(lax.axis_s...]
    unnamed x20 -> x2, local copies, waits for them, and re-layouts: 7.25 us -> 0.01 us
    pallas_call x1, Pallas kernels: 6.88 us -> 3.65 us  [shards(): pl.pallas_call(functools.partial(finish_kernel, levels), out_shape=f32(sl...]
  transfers between devices with their start and end apart: 10 -> 17, of which waited for: 5 -> 6; matrix products, arithmetic and copies ran while one was open for 0% -> 0% of each run, Pallas kernels for 21% -> 27%
where the time goes in v2:
time: 111 us; the launch traced here: 110 us
  Pallas kernels  60.1 us (54%)
  waiting for transfers between devices  28.9 us (26%)
  starting transfers between devices  20.5 us (18%)
    ppermute x17, waiting for transfers between devices, swapped(): lax.ppermute(shard, axis, [(i, i ^ 1 << stride) for i in range(lax.axis_s...  28.9 us
    pallas_call x1, Pallas kernels, shards(): pl.pallas_call(leaf_kernel, out_shape=(near(R, R), near(R, 2 * R), near(R...  22.9 us
    pallas_call x5, Pallas kernels, invert(): pl.pallas_call(functools.partial(invert_kernel, level), out_shape=(near(2...  22.5 us
    ppermute x17, starting transfers between devices, swapped(): lax.ppermute(shard, axis, [(i, i ^ 1 << stride) for i in range(lax.axis_s...  20.5 us
    pallas_call x12, Pallas kernels, condense(): pl.pallas_call(functools.partial(condense_kernel, level, levels, group),...  11.1 us
    pallas_call x1, Pallas kernels, shards(): pl.pallas_call(functools.partial(finish_kernel, levels), out_shape=f32(sl...  3.65 us
  transfers between devices with their start and end apart: 17, of which 6 were waited for; matrix products, arithmetic and copies ran while one was open for 0% of the time, Pallas kernels for 27%

profile of v2, /device:TPU:0, one launch (start us, length us, event | category | flops | bytes accessed | tf_op | source)
XLA Modules:
  0.0 110.4 jit_solution(17094601207054703489)
XLA Ops:
  0.8 22.9 %leaf.1 = (f32[128,128]{1,0:T(8,128)S(1)}, f32[128,256]{1,0:T(8,128)S(1)}, f32[128,2176]{1,0:T(8,128)S(1)}, f32[1024,1024]{1,0:T(8,128)S(1)}, f32[768,1024]{1,0:T(8,128)S(1)}) custom-call(s32[1]{0:T(128)S(6)} %copy.7.count_ref, f32[3,1024]{1,0:T(4,128)} %points_ref.1, s32[1,1024]{1,0:T(1,128)} %order_ref.1, f32[1024,640]{1,0:T(8,128)} %basis_ref.1, ...), custom_call_target="tpu_custom_call" | custom-call | tf_op jit(solution)/shard_map/leaf/pallas_call | solution.py:287
  24.3 2.4 %collective-permute-done.1.sibling_ref = f32[128,128]{1,0:T(8,128)S(1)} collective-permute-done((f32[128,128]{1,0:T(8,128)S(1)}, f32[128,128]{1,0:T(8,128)S(1)}, u32[]{:S(2)}, u32[]{:S(2)}) %collective-permute-start.1) | collective-permute-done | bytes 65568 | tf_op jit(solution)/shard_map/ppermute | solution.py:235
  26.8 3.9 %shard_map.64 = (f32[256,256]{1,0:T(8,128)S(1)}, f32[8,128]{1,0:T(8,128)S(1)}) custom-call(f32[128,128]{1,0:T(8,128)S(1)} %get-tuple-element.70.own_ref, f32[128,128]{1,0:T(8,128)S(1)} %collective-permute-done.1.sibling_ref, f32[5,256,256]{2,1,0:T(8,128)S(1)} %copy-done, f32[8,128]{1,0:T(8,128)S(1)} %broadcast_in_dim.3.after_ref), custom_call_target="tpu_custom_call" | custom-call | tf_op jit(solution)/shard_map/pallas_call | solution.py:314
  31.4 2.3 %shard_map.66 = (f32[128,256]{1,0:T(8,128)S(1)}, f32[128,384]{1,0:T(8,128)S(1)}, f32[128,512]{1,0:T(8,128)S(1)}, f32[128,512]{1,0:T(8,128)S(1)}, f32[128,256]{1,...) custom-call(f32[128,2176]{1,0:T(8,128)S(1)} %get-tuple-element.74.re, ...), custom_call_target="tpu_custom_call" | custom-call | tf_op jit(solution)/shard_map/pallas_call | solution.py:328
  33.7 2.4 %collective-permute-start.5 = (f32[128,384]{1,0:T(8,128)S(1)}, f32[128,384]{1,0:T(8,128)S(1)}, u32[]{:S(2)}, u32[]{:S(2)}) collective-permute-start(f32[128,384]{1,0:T(8,128)S(1)} %get-tuple-element.87.refs_0_), channel_id=1, source_target_pairs={{0,2},{1,3},{2,0},{3,1},{4,6},{5,7},{6,4},{7,5},{8,10},{9,11},{10,... | collective-permute-start | bytes 589832 | tf_op jit(solution)/shard_map/ppermute | solution.py:235
  36.2 2.0 %collective-permute-start.6 = (f32[128,512]{1,0:T(8,128)S(1)}, f32[128,512]{1,0:T(8,128)S(1)}, u32[]{:S(2)}, u32[]{:S(2)}) collective-permute-start(f32[128,512]{1,0:T(8,128)S(1)} %get-tuple-element.91.refs_0_), channel_id=1, source_target_pairs={{0,2},{1,3},{2,0},{3,1},{4,6},{5,7},{6,4},{7,5},{8,10},{9,11},{10,... | collective-permute-start | bytes 786440 | tf_op jit(solution)/shard_map/ppermute | solution.py:235
  38.2 13.2 %collective-permute-done.4.sibling_ref = f32[128,128]{1,0:T(8,128)S(1)} collective-permute-done((f32[128,128]{1,0:T(8,128)S(1)}, f32[128,128]{1,0:T(8,128)S(1)}, u32[]{:S(2)}, u32[]{:S(2)}) %collective-permute-start.4) | collective-permute-done | bytes 65568 | tf_op jit(solution)/shard_map/ppermute | solution.py:235
  51.4 4.4 %shard_map.67 = (f32[256,256]{1,0:T(8,128)S(1)}, f32[8,128]{1,0:T(8,128)S(1)}) custom-call(f32[128,128]{1,0:T(8,128)S(1)} %get-tuple-element.82.own_ref, f32[128,128]{1,0:T(8,128)S(1)} %collective-permute-done.4.sibling_ref, f32[5,256,256]{2,1,0:T(8,128)S(1)} %copy-done, f32[8,128]{1,0:T(8,128)S(1)} %get-tuple-element.83.after_ref), custom_call_target="tpu_custom_call" | custom-call | tf_op jit(solution)/shard_map/pallas_call | solution.py:314
  57.2 2.3 %collective-permute-start.7 = (f32[128,256]{1,0:T(8,128)S(1)}, f32[128,256]{1,0:T(8,128)S(1)}, u32[]{:S(2)}, u32[]{:S(2)}) collective-permute-start(f32[128,256]{1,0:T(8,128)S(1)} %get-tuple-element.93.refs_0_), channel_id=1, source_target_pairs={{0,4},{4,0},{8,12},{12,8},{16,20},{20,16},{24,28},{28,24},{1,5},{5... | collective-permute-start | bytes 393224 | tf_op jit(solution)/shard_map/ppermute | solution.py:235
  59.7 1.3 %collective-permute-start.8 = (f32[128,128]{1,0:T(8,128)S(1)}, f32[128,128]{1,0:T(8,128)S(1)}, u32[]{:S(2)}, u32[]{:S(2)}) collective-permute-start(f32[128,128]{1,0:T(8,128)S(1)} %get-tuple-element.94.own_ref), channel_id=1, source_target_pairs={{0,4},{4,0},{8,12},{12,8},{16,20},{20,16},{24,28},{28,24},{1,5},{5... | collective-permute-start | bytes 196616 | tf_op jit(solution)/shard_map/ppermute | solution.py:235
  61.0 3.0 %collective-permute-done.8.sibling_ref = f32[128,128]{1,0:T(8,128)S(1)} collective-permute-done((f32[128,128]{1,0:T(8,128)S(1)}, f32[128,128]{1,0:T(8,128)S(1)}, u32[]{:S(2)}, u32[]{:S(2)}) %collective-permute-start.8) | collective-permute-done | bytes 65568 | tf_op jit(solution)/shard_map/ppermute | solution.py:235
  64.0 4.6 %shard_map.70 = (f32[256,256]{1,0:T(8,128)S(1)}, f32[8,128]{1,0:T(8,128)S(1)}) custom-call(f32[128,128]{1,0:T(8,128)S(1)} %get-tuple-element.94.own_ref, f32[128,128]{1,0:T(8,128)S(1)} %collective-permute-done.8.sibling_ref, f32[5,256,256]{2,1,0:T(8,128)S(1)} %copy-done, f32[8,128]{1,0:T(8,128)S(1)} %get-tuple-element.95.after_ref), custom_call_target="tpu_custom_call" | custom-call | tf_op jit(solution)/shard_map/pallas_call | solution.py:314
  70.1 1.8 %collective-permute-start.10 = (f32[128,384]{1,0:T(8,128)S(1)}, f32[128,384]{1,0:T(8,128)S(1)}, u32[]{:S(2)}, u32[]{:S(2)}) collective-permute-start(f32[128,384]{1,0:T(8,128)S(1)} %get-tuple-element.105.refs_0_), channel_id=1, source_target_pairs={{0,4},{4,0},{8,12},{12,8},{16,20},{20,16},{24,28},{28,24},{1,5},{5... | collective-permute-start | bytes 589832 | tf_op jit(solution)/shard_map/ppermute | solution.py:235
  73.2 4.8 %collective-permute-done.10.refs_1_ = f32[128,384]{1,0:T(8,128)S(1)} collective-permute-done((f32[128,384]{1,0:T(8,128)S(1)}, f32[128,384]{1,0:T(8,128)S(1)}, u32[]{:S(2)}, u32[]{:S(2)}) %collective-permute-start.10) | collective-permute-done | bytes 196640 | tf_op jit(solution)/shard_map/ppermute | solution.py:235
  78.6 1.9 %collective-permute-start.12 = (f32[128,256]{1,0:T(8,128)S(1)}, f32[128,256]{1,0:T(8,128)S(1)}, u32[]{:S(2)}, u32[]{:S(2)}) collective-permute-start(f32[128,256]{1,0:T(8,128)S(1)} %get-tuple-element.111.refs_0_), channel_id=1, source_target_pairs={{0,8},{4,12},{8,0},{12,4},{16,24},{20,28},{24,16},{28,20},{1,9},{5... | collective-permute-start | bytes 393224 | tf_op jit(solution)/shard_map/ppermute | solution.py:235
  80.7 4.1 %collective-permute-done.13.sibling_ref = f32[128,128]{1,0:T(8,128)S(1)} collective-permute-done((f32[128,128]{1,0:T(8,128)S(1)}, f32[128,128]{1,0:T(8,128)S(1)}, u32[]{:S(2)}, u32[]{:S(2)}) %collective-permute-start.13) | collective-permute-done | bytes 65568 | tf_op jit(solution)/shard_map/ppermute | solution.py:235
  84.8 4.8 %shard_map.75 = (f32[256,256]{1,0:T(8,128)S(1)}, f32[8,128]{1,0:T(8,128)S(1)}) custom-call(f32[128,128]{1,0:T(8,128)S(1)} %get-tuple-element.112.own_ref, f32[128,128]{1,0:T(8,128)S(1)} %collective-permute-done.13.sibling_ref, f32[5,256,256]{2,1,0:T(8,128)S(1)} %copy-done, f32[8,128]{1,0:T(8,128)S(1)} %get-tuple-element.113.after_ref), custom_call_target="tpu_custom_call" | custom-call | tf_op jit(solution)/shard_map/pallas_call | solution.py:314
  91.2 1.4 %collective-permute-start.14 = (f32[128,256]{1,0:T(8,128)S(1)}, f32[128,256]{1,0:T(8,128)S(1)}, u32[]{:S(2)}, u32[]{:S(2)}) collective-permute-start(f32[128,256]{1,0:T(8,128)S(1)} %get-tuple-element.119.refs_0_), channel_id=1, source_target_pairs={{0,8},{4,12},{8,0},{12,4},{16,24},{20,28},{24,16},{28,20},{1,9},{5... | collective-permute-start | bytes 393224 | tf_op jit(solution)/shard_map/ppermute | solution.py:235
  92.7 3.0 %collective-permute-start.16 = (f32[128,128]{1,0:T(8,128)S(1)}, f32[128,128]{1,0:T(8,128)S(1)}, u32[]{:S(2)}, u32[]{:S(2)}) collective-permute-start(f32[128,128]{1,0:T(8,128)S(1)} %get-tuple-element.124.own_ref), channel_id=1, source_target_pairs={{0,16},{4,20},{8,24},{12,28},{16,0},{20,4},{24,8},{28,12},{1,17},{... | collective-permute-start | bytes 196616 | tf_op jit(solution)/shard_map/ppermute | solution.py:235
  95.6 1.3 %collective-permute-done.14.refs_1_ = f32[128,256]{1,0:T(8,128)S(1)} collective-permute-done((f32[128,256]{1,0:T(8,128)S(1)}, f32[128,256]{1,0:T(8,128)S(1)}, u32[]{:S(2)}, u32[]{:S(2)}) %collective-permute-start.14) | collective-permute-done | bytes 131104 | tf_op jit(solution)/shard_map/ppermute | solution.py:235
  97.9 3.0 %collective-permute-start.15 = (f32[128,128]{1,0:T(8,128)S(1)}, f32[128,128]{1,0:T(8,128)S(1)}, u32[]{:S(2)}, u32[]{:S(2)}) collective-permute-start(f32[128,128]{1,0:T(8,128)S(1)} %get-tuple-element.123.refs_0_), channel_id=1, source_target_pairs={{0,16},{4,20},{8,24},{12,28},{16,0},{20,4},{24,8},{28,12},{1,17},{... | collective-permute-start | bytes 196616 | tf_op jit(solution)/shard_map/ppermute | solution.py:235
  100.9 4.8 %shard_map.79 = (f32[256,256]{1,0:T(8,128)S(1)}, f32[8,128]{1,0:T(8,128)S(1)}) custom-call(f32[128,128]{1,0:T(8,128)S(1)} %get-tuple-element.124.own_ref, f32[128,128]{1,0:T(8,128)S(1)} %collective-permute-done.16.sibling_ref, f32[5,256,256]{2,1,0:T(8,128)S(1)} %copy-done, f32[8,128]{1,0:T(8,128)S(1)} %get-tuple-element.125.after_ref), custom_call_target="tpu_custom_call" | custom-call | tf_op jit(solution)/shard_map/pallas_call | solution.py:314
  105.8 1.0 shard_map.80
  106.8 3.6 %finish.1 = f32[1024,128]{1,0:T(8,128)} custom-call(f32[768,1024]{1,0:T(8,128)S(1)} %get-tuple-element.67.rows_ref, f32[1024,1024]{1,0:T(8,128)S(1)} %get-tuple-element.68.factor_ref, f32[128,128]{1,0:T(8,128)S(1)} %get-tuple-element.73.refs_0_, f32[128,128]{1,0:T(8,128)S(1)} %get-tuple-element.77.refs_1_, f32[128,128]{1,0:T(8,128)S(1)} %get-tuple-element.78.refs_2_, ...), custom_call_target="tpu_custom_call" | custom-call | tf_op jit(solution)/shard_map/finish/pallas_call | solution.py:356
  (32 shorter events, 9.3 us)
Async XLA Ops:
  0.0 26.8 %copy-start = (f32[5,256,256]{2,1,0:T(8,128)S(1)}, f32[5,256,256]{2,1,0:T(8,128)}, u32[]{:S(2)}) copy-start(f32[5,256,256]{2,1,0:T(8,128)} %refs_3_.23) | copy-start | bytes 3932164
  23.6 7.7 %collective-permute-start.2 = (f32[128,2176]{1,0:T(8,128)S(1)}, f32[128,2176]{1,0:T(8,128)S(1)}, u32[]{:S(2)}, u32[]{:S(2)}) collective-permute-start(f32[128,2176]{1,0:T(8,128)S(1)} %get-tuple-element.74.refs_0_), channel_id=1, source_target_pairs={{0,1},{1,0},{2,3},{3,2},{4,5},{5,4},{6,7},{7,6},{8,9},{9,8},{10,11... | collective-permute-start | bytes 3342344 | tf_op jit(solution)/shard_map/ppermute | solution.py:235
  23.8 6.9 %collective-permute-start = (f32[128,256]{1,0:T(8,128)S(1)}, f32[128,256]{1,0:T(8,128)S(1)}, u32[]{:S(2)}, u32[]{:S(2)}) collective-permute-start(f32[128,256]{1,0:T(8,128)S(1)} %get-tuple-element.69.refs_0_), channel_id=1, source_target_pairs={{0,1},{1,0},{2,3},{3,2},{4,5},{5,4},{6,7},{7,6},{8,9},{9,8},{10,11... | collective-permute-start | bytes 393224 | tf_op jit(solution)/shard_map/ppermute | solution.py:235
  24.2 2.5 %collective-permute-start.1 = (f32[128,128]{1,0:T(8,128)S(1)}, f32[128,128]{1,0:T(8,128)S(1)}, u32[]{:S(2)}, u32[]{:S(2)}) collective-permute-start(f32[128,128]{1,0:T(8,128)S(1)} %get-tuple-element.70.own_ref), channel_id=1, source_target_pairs={{0,1},{1,0},{2,3},{3,2},{4,5},{5,4},{6,7},{7,6},{8,9},{9,8},{10,11... | collective-permute-start | bytes 196616 | tf_op jit(solution)/shard_map/ppermute | solution.py:235
  33.7 22.7 %collective-permute-start.5 = (f32[128,384]{1,0:T(8,128)S(1)}, f32[128,384]{1,0:T(8,128)S(1)}, u32[]{:S(2)}, u32[]{:S(2)}) collective-permute-start(f32[128,384]{1,0:T(8,128)S(1)} %get-tuple-element.87.refs_0_), channel_id=1, source_target_pairs={{0,2},{1,3},{2,0},{3,1},{4,6},{5,7},{6,4},{7,5},{8,10},{9,11},{10,... | collective-permute-start | bytes 589832 | tf_op jit(solution)/shard_map/ppermute | solution.py:235
  36.1 19.6 %collective-permute-start.3 = (f32[128,256]{1,0:T(8,128)S(1)}, f32[128,256]{1,0:T(8,128)S(1)}, u32[]{:S(2)}, u32[]{:S(2)}) collective-permute-start(f32[128,256]{1,0:T(8,128)S(1)} %get-tuple-element.81.refs_0_), channel_id=1, source_target_pairs={{0,2},{1,3},{2,0},{3,1},{4,6},{5,7},{6,4},{7,5},{8,10},{9,11},{10,... | collective-permute-start | bytes 393224 | tf_op jit(solution)/shard_map/ppermute | solution.py:235
  36.2 33.2 %collective-permute-start.6 = (f32[128,512]{1,0:T(8,128)S(1)}, f32[128,512]{1,0:T(8,128)S(1)}, u32[]{:S(2)}, u32[]{:S(2)}) collective-permute-start(f32[128,512]{1,0:T(8,128)S(1)} %get-tuple-element.91.refs_0_), channel_id=1, source_target_pairs={{0,2},{1,3},{2,0},{3,1},{4,6},{5,7},{6,4},{7,5},{8,10},{9,11},{10,... | collective-permute-start | bytes 786440 | tf_op jit(solution)/shard_map/ppermute | solution.py:235
  38.2 13.2 %collective-permute-start.4 = (f32[128,128]{1,0:T(8,128)S(1)}, f32[128,128]{1,0:T(8,128)S(1)}, u32[]{:S(2)}, u32[]{:S(2)}) collective-permute-start(f32[128,128]{1,0:T(8,128)S(1)} %get-tuple-element.82.own_ref), channel_id=1, source_target_pairs={{0,2},{1,3},{2,0},{3,1},{4,6},{5,7},{6,4},{7,5},{8,10},{9,11},{10,... | collective-permute-start | bytes 196616 | tf_op jit(solution)/shard_map/ppermute | solution.py:235
  57.2 11.4 %collective-permute-start.7 = (f32[128,256]{1,0:T(8,128)S(1)}, f32[128,256]{1,0:T(8,128)S(1)}, u32[]{:S(2)}, u32[]{:S(2)}) collective-permute-start(f32[128,256]{1,0:T(8,128)S(1)} %get-tuple-element.93.refs_0_), channel_id=1, source_target_pairs={{0,4},{4,0},{8,12},{12,8},{16,20},{20,16},{24,28},{28,24},{1,5},{5... | collective-permute-start | bytes 393224 | tf_op jit(solution)/shard_map/ppermute | solution.py:235
  59.5 12.4 %collective-permute-start.9 = (f32[128,512]{1,0:T(8,128)S(1)}, f32[128,512]{1,0:T(8,128)S(1)}, u32[]{:S(2)}, u32[]{:S(2)}) collective-permute-start(f32[128,512]{1,0:T(8,128)S(1)} %get-tuple-element.100.refs_0_), channel_id=1, source_target_pairs={{0,2},{1,3},{2,0},{3,1},{4,6},{5,7},{6,4},{7,5},{8,10},{9,11},{10,... | collective-permute-start | bytes 786440 | tf_op jit(solution)/shard_map/ppermute | solution.py:235
  59.7 4.3 %collective-permute-start.8 = (f32[128,128]{1,0:T(8,128)S(1)}, f32[128,128]{1,0:T(8,128)S(1)}, u32[]{:S(2)}, u32[]{:S(2)}) collective-permute-start(f32[128,128]{1,0:T(8,128)S(1)} %get-tuple-element.94.own_ref), channel_id=1, source_target_pairs={{0,4},{4,0},{8,12},{12,8},{16,20},{20,16},{24,28},{28,24},{1,5},{5... | collective-permute-start | bytes 196616 | tf_op jit(solution)/shard_map/ppermute | solution.py:235
  70.1 7.8 %collective-permute-start.10 = (f32[128,384]{1,0:T(8,128)S(1)}, f32[128,384]{1,0:T(8,128)S(1)}, u32[]{:S(2)}, u32[]{:S(2)}) collective-permute-start(f32[128,384]{1,0:T(8,128)S(1)} %get-tuple-element.105.refs_0_), channel_id=1, source_target_pairs={{0,4},{4,0},{8,12},{12,8},{16,20},{20,16},{24,28},{28,24},{1,5},{5... | collective-permute-start | bytes 589832 | tf_op jit(solution)/shard_map/ppermute | solution.py:235
  72.9 17.4 %collective-permute-start.11 = (f32[128,384]{1,0:T(8,128)S(1)}, f32[128,384]{1,0:T(8,128)S(1)}, u32[]{:S(2)}, u32[]{:S(2)}) collective-permute-start(f32[128,384]{1,0:T(8,128)S(1)} %get-tuple-element.109.refs_0_), channel_id=1, source_target_pairs={{0,4},{4,0},{8,12},{12,8},{16,20},{20,16},{24,28},{28,24},{1,5},{5... | collective-permute-start | bytes 589832 | tf_op jit(solution)/shard_map/ppermute | solution.py:235
  78.6 11.0 %collective-permute-start.12 = (f32[128,256]{1,0:T(8,128)S(1)}, f32[128,256]{1,0:T(8,128)S(1)}, u32[]{:S(2)}, u32[]{:S(2)}) collective-permute-start(f32[128,256]{1,0:T(8,128)S(1)} %get-tuple-element.111.refs_0_), channel_id=1, source_target_pairs={{0,8},{4,12},{8,0},{12,4},{16,24},{20,28},{24,16},{28,20},{1,9},{5... | collective-permute-start | bytes 393224 | tf_op jit(solution)/shard_map/ppermute | solution.py:235
  80.5 4.3 %collective-permute-start.13 = (f32[128,128]{1,0:T(8,128)S(1)}, f32[128,128]{1,0:T(8,128)S(1)}, u32[]{:S(2)}, u32[]{:S(2)}) collective-permute-start(f32[128,128]{1,0:T(8,128)S(1)} %get-tuple-element.112.own_ref), channel_id=1, source_target_pairs={{0,8},{4,12},{8,0},{12,4},{16,24},{20,28},{24,16},{28,20},{1,9},{5... | collective-permute-start | bytes 196616 | tf_op jit(solution)/shard_map/ppermute | solution.py:235
  91.2 5.7 %collective-permute-start.14 = (f32[128,256]{1,0:T(8,128)S(1)}, f32[128,256]{1,0:T(8,128)S(1)}, u32[]{:S(2)}, u32[]{:S(2)}) collective-permute-start(f32[128,256]{1,0:T(8,128)S(1)} %get-tuple-element.119.refs_0_), channel_id=1, source_target_pairs={{0,8},{4,12},{8,0},{12,4},{16,24},{20,28},{24,16},{28,20},{1,9},{5... | collective-permute-start | bytes 393224 | tf_op jit(solution)/shard_map/ppermute | solution.py:235
  92.7 8.3 %collective-permute-start.16 = (f32[128,128]{1,0:T(8,128)S(1)}, f32[128,128]{1,0:T(8,128)S(1)}, u32[]{:S(2)}, u32[]{:S(2)}) collective-permute-start(f32[128,128]{1,0:T(8,128)S(1)} %get-tuple-element.124.own_ref), channel_id=1, source_target_pairs={{0,16},{4,20},{8,24},{12,28},{16,0},{20,4},{24,8},{28,12},{1,17},{... | collective-permute-start | bytes 196616 | tf_op jit(solution)/shard_map/ppermute | solution.py:235
  97.9 7.8 %collective-permute-start.15 = (f32[128,128]{1,0:T(8,128)S(1)}, f32[128,128]{1,0:T(8,128)S(1)}, u32[]{:S(2)}, u32[]{:S(2)}) collective-permute-start(f32[128,128]{1,0:T(8,128)S(1)} %get-tuple-element.123.refs_0_), channel_id=1, source_target_pairs={{0,16},{4,20},{8,24},{12,28},{16,0},{20,4},{24,8},{28,12},{1,17},{... | collective-permute-start | bytes 196616 | tf_op jit(solution)/shard_map/ppermute | solution.py:235

commit v3 on v2

--- a/solution.py
+++ b/solution.py
@@ -38,6 +38,11 @@
     size = matrix.shape[0]
     eye = identity(size)
     low = 1.0 / jnp.max(jnp.sum(jnp.abs(matrix), axis=0))
+    slack = 1e-3 if refine else 3e-6
+    z = matrix * low
+    scale = 4.0 / ((1.0 + low) * (1.0 + low))
+    shift = 1.0 + low
+    first = (low * scale, (scale * low) * (shift * eye - z), scale * (shift * z - nn(z, z)))
 
     def step(carry):
         low, x, z = carry
@@ -49,9 +54,7 @@
             scale * (shift * z - nn(z, z)),
         )
 
-    _, x, _ = lax.while_loop(
-        lambda carry: carry[0] < 1.0 - 6e-7, step, (low, eye * low, matrix * low)
-    )
+    _, x, _ = lax.while_loop(lambda carry: carry[0] < 1.0 - slack, step, first)
     if refine:
         x = x + nn(x, eye - nn(matrix, x, HIGHEST))
     return x
@@ -129,17 +132,19 @@
                 factor_ref[j * tile :, js] -= nt(lower[at:], panel[at : at + tile])
             rows_ref[:, (k + 1) * tile :] -= nt(own, lower)
         weighted_ref[:, ks] = nn(own, x)
-    for m in range(levels):
-        column = nt(weighted_ref[m * R :, :], rows_ref[m * R : (m + 1) * R, :])
-        if m == 0:
-            head_ref[...] = column[:R]
-        for c in range(max(m, 1), blocks):
-            piece = column[(c - m) * R : (c - m + 1) * R]
-            if c == 1:
-                near_rows_ref[:, m * R : (m + 1) * R] = piece
-            else:
-                at = (row_start(levels, 0, 2, c) + m) * R
-                far_rows_ref[:, at : at + R] = piece
+    for pair in range(0, levels, 2):
+        wide = range(pair, min(pair + 2, levels))
+        columns = nt(weighted_ref[pair * R :, :], rows_ref[pair * R : (wide[-1] + 1) * R, :])
+        for m in wide:
+            if m == 0:
+                head_ref[...] = columns[:R, :R]
+            for c in range(max(m, 1), blocks):
+                piece = columns[(c - pair) * R : (c - pair + 1) * R, (m - pair) * R : (m - pair + 1) * R]
+                if c == 1:
+                    near_rows_ref[:, m * R : (m + 1) * R] = piece
+                else:
+                    at = (row_start(levels, 0, 2, c) + m) * R
+                    far_rows_ref[:, at : at + R] = piece
 
 
 def row_blocks(levels, level, row):
@@ -157,51 +162,105 @@
     return lax.axis_index("leaf") >> (level - sub_bits) & 1
 
 
-def invert_kernel(level, own_ref, sibling_ref, factor_ref, after_ref, inverse_ref, token_ref):
+def invert_kernel(level, levels, own_ref, *refs):
+    sibling_refs, (factor_ref, _, inverse_ref, token_ref) = refs[:-4], refs[-4:]
+    sibling = sibling_refs[0][...]
+    if len(sibling_refs) > 1:
+        sibling = chosen_row(levels, level, sibling, sibling_refs[1][...])
     side = side_of(level)
     mine = factor_ref[level, pl.ds(pl.multiple_of(side * R, R), R), :]
     theirs = factor_ref[level, pl.ds(pl.multiple_of((1 - side) * R, R), R), :]
     pair = jnp.concatenate([mine, theirs], axis=0)
-    inner = jnp.concatenate([nn(own_ref[...], mine), nn(sibling_ref[...], theirs)], axis=0)
+    inner = jnp.concatenate([nn(own_ref[...], mine), nn(sibling, theirs)], axis=0)
     coupled = identity(2 * R) + nn(pair.T, inner)
     coupled = 0.5 * (coupled + coupled.T)
     inverse_ref[...] = inverse(coupled, True)
     token_ref[...] = jnp.zeros_like(token_ref)
 
 
+def groups_of(levels, level):
+    if level == 0:
+        return [(1,), tuple(range(2, levels + 1))]
+    if level == levels - 1:
+        return [(levels,)]
+    return [(row,) for row in range(level + 1, levels - 1)] + [(levels - 1, levels)]
+
+
+def is_split(levels, level, group):
+    return level > 0 and (len(group) == 2 or level == levels - 1)
+
+
+def has_portion(levels, level, group):
+    return is_split(levels, level, group) and group[-1] == levels
+
+
+def chosen_row(levels, row, direct, passed_on):
+    return jnp.where(side_of(0) == row - (levels - 1), direct, passed_on)
+
+
+def width_of(levels, level, group):
+    return row_start(levels, level, group[0], group[-1] + 1) * R
+
+
+def next_groups(levels, level, group):
+    found = []
+    if group[0] == level + 1 < levels:
+        found.append((level + 1,))
+    if level < levels - 1:
+        found += [one for one in groups_of(levels, level + 1) if set(one) <= set(group)]
+    return found
+
+
 def condense_kernel(level, levels, group, *refs):
-    own_ref, sibling_ref, inverse_ref, factor_ref = refs[:4]
-    known = group[0] - level - 1
-    forcing_refs, refs = refs[4 : 4 + known], refs[4 + known :]
-    refs = refs[1:]
-    passed = [row for row in group if row > level + 1 or level < levels - 1]
-    next_refs, refs = refs[: len(passed)], refs[len(passed) :]
-    new_forcing_refs, gain_refs, token_ref = refs[: len(group)], refs[len(group) : -1], refs[-1]
+    refs = list(refs)
+    take = lambda count: [refs.pop(0) for _ in range(count)]
+    (own_ref,) = take(1)
+    sibling_refs = take(2 if is_split(levels, level, group) else 1)
+    inverse_ref, factor_ref = take(2)
+    forcing_refs = take(group[0] - level - 1)
+    take(1)
+    after = next_groups(levels, level, group)
+    targets = [take(2 if has_portion(levels, level + 1, one) else 1) for one in after]
+    new_forcing_refs, gain_refs = take(len(group)), take(len(group))
+    (token_ref,) = refs
     side = side_of(level)
     mine = factor_ref[level, pl.ds(pl.multiple_of(side * R, R), R), :]
     theirs = factor_ref[level, pl.ds(pl.multiple_of((1 - side) * R, R), R), :]
     pair = jnp.concatenate([mine, theirs], axis=0)
-    starts = [row_start(levels, level, group[0], row) * R for row in group]
-    own_side = jnp.concatenate([own_ref[:, at : at + R] for at in starts], axis=0)
-    other_side = jnp.concatenate([sibling_ref[:, at : at + R] for at in starts], axis=0)
+    own, sibling = {}, {}
+    for row in group:
+        at = row_start(levels, level, group[0], row) * R
+        width = row_blocks(levels, level, row) * R
+        own[row] = own_ref[:, at : at + width]
+        if is_split(levels, level, group):
+            sibling[row] = chosen_row(levels, row, sibling_refs[0][...], sibling_refs[1][...])
+        else:
+            sibling[row] = sibling_refs[0][:, at : at + width]
+    own_side = jnp.concatenate([own[row][:, :R] for row in group], axis=0)
+    other_side = jnp.concatenate([sibling[row][:, :R] for row in group], axis=0)
     forcing = nn(jnp.concatenate([own_side, other_side], axis=1), pair)
     coefficients = nn(forcing, inverse_ref[...])
-    gains = nt(coefficients, mine)
     every = [ref[...] for ref in forcing_refs]
     for index, row in enumerate(group):
         piece = forcing[index * R : (index + 1) * R]
         new_forcing_refs[index][...] = piece
+        every.append(piece)
+    reduced = {}
+    for index, row in enumerate(group):
+        width = row_blocks(levels, level, row) - 1
+        if width > 0:
+            total = own[row][:, R:] + sibling[row][:, R:]
+            part = coefficients[index * R : (index + 1) * R]
+            reduced[row] = total - nt(part, jnp.concatenate(every[:width], axis=0))
+    for one, target in zip(after, targets):
+        for row in one:
+            at = 0 if len(one) == 1 else row_start(levels, level + 1, one[0], row) * R
+            target[0][:, at : at + reduced[row].shape[1]] = reduced[row]
+        if has_portion(levels, level + 1, one):
+            target[1][...] = chosen_row(levels, levels, reduced[levels], reduced[levels - 1])
+    gains = nt(coefficients, mine)
+    for index in range(len(group)):
         gain_refs[index][...] = gains[index * R : (index + 1) * R]
-        every.append(piece)
-    for index, row in enumerate(group):
-        width = (row_blocks(levels, level, row) - 1) * R
-        if width == 0:
-            continue
-        at = starts[index] + R
-        total = own_ref[:, at : at + width] + sibling_ref[:, at : at + width]
-        against = jnp.concatenate(every[: width // R], axis=0)
-        part = coefficients[index * R : (index + 1) * R]
-        next_refs[index][...] = total - nt(part, against)
     token_ref[...] = jnp.zeros_like(token_ref)
 
 
@@ -265,16 +324,12 @@
 
 
 def schedule(levels):
-    others = tuple(range(2, levels + 1))
-    plan = [("invert", 0), ("condense", 0, (1,)), ("condense", 0, others)]
+    first, rest = groups_of(levels, 0)
+    plan = [("invert", 0), ("condense", 0, first), ("condense", 0, rest)]
     for level in range(1, levels):
-        plan += [("invert", level), ("condense", level, (level + 1,))]
-        for at in range(1, level + 1):
-            if at > 1 and level + 3 <= levels:
-                plan.append(("condense", at - 1, (level + 3,)))
-            if level + 2 <= levels:
-                plan.append(("condense", at, (level + 2,)))
-    return list(dict.fromkeys(plan))
+        plan.append(("invert", level))
+        plan += [("condense", level, rows) for rows in groups_of(levels, level)]
+    return plan
 
 
 def shards(points, order, counts, basis, right_side, coupling):
@@ -304,42 +359,62 @@
     gains = {}
     forcing = {}
     sent = {}
+    waiting = {}
     inverted = {}
     chain = [jnp.zeros((8, R), jnp.float32)]
 
-    def send(level, group, value):
-        sent[level, group] = (value, hold(pair_swap(value, level, sub_bits)))
+    def send(level, group, own, portion=None):
+        if portion is None and is_split(levels, level, group):
+            waiting[level] = own
+            return
+        arrived = [hold(pair_swap(own if portion is None else portion, level, sub_bits))]
+        if portion is not None:
+            arrived.append(hold(pair_swap(arrived[0], 0, sub_bits)))
+        sent[level, group] = (own, *arrived)
+        if level in waiting:
+            sent[level, (level,)] = (waiting[level], *arrived)
 
     def invert(level):
+        operands = [*sent[level, (level,)], coupling, hold(chain[0])]
         inverted[level], chain[0] = pl.pallas_call(
-            functools.partial(invert_kernel, level),
+            functools.partial(invert_kernel, level, levels),
             out_shape=(near(2 * R, 2 * R), token),
-            in_specs=[VMEM] * 4,
+            in_specs=[VMEM] * len(operands),
             out_specs=[VMEM] * 2,
             compiler_params=LIMIT,
-        )(*sent[level, (level,)], coupling, hold(chain[0]))
+        )(*operands)
 
     def condense(level, group):
         known = range(level + 1, group[0])
-        widths = [row_blocks(levels, level, row) - 1 for row in group]
-        shapes = [near(R, width * R) for width in widths if width > 0]
+        after = next_groups(levels, level, group)
+        shapes = []
+        for one in after:
+            width = R if one == (level + 1,) else width_of(levels, level + 1, one)
+            shapes.append(near(R, width))
+            if has_portion(levels, level + 1, one):
+                shapes.append(near(R, width // len(one)))
         passed = len(shapes)
         shapes += [near(R, 2 * R)] * len(group) + [near(R, R)] * len(group) + [token]
+        operands = [
+            *sent[level, group], inverted[level], coupling,
+            *[forcing[level, row] for row in known], hold(chain[0]),
+        ]
         outs = pl.pallas_call(
             functools.partial(condense_kernel, level, levels, group),
             out_shape=shapes,
-            in_specs=[VMEM] * (5 + len(known)),
+            in_specs=[VMEM] * len(operands),
             out_specs=[VMEM] * len(shapes),
             compiler_params=LIMIT,
-        )(
-            *sent[level, group], inverted[level], coupling,
-            *[forcing[level, row] for row in known], hold(chain[0]),
-        )
+        )(*operands)
         chain[0] = outs[-1]
         for index, row in enumerate(group):
             forcing[level, row] = outs[passed + index]
             gains[level, row] = outs[passed + len(group) + index]
-        return [(level + 1, (group[index],), outs[index]) for index in range(passed)]
+        made = list(outs[:passed])
+        return [
+            (level + 1, one, *[made.pop(0) for _ in range(2 if has_portion(levels, level + 1, one) else 1)])
+            for one in after
+        ]
 
     others = tuple(range(2, levels + 1))
     send(0, (0,), head)

time: 111 us -> 112 us (level)
  waiting for transfers between devices: 28.9 us -> 39.2 us
  Pallas kernels: 60.1 us -> 54.9 us
  starting transfers between devices: 20.5 us -> 16.3 us
    ppermute x17, waiting for transfers between devices: 28.9 us -> 39.2 us  [swapped(): lax.ppermute(shard, axis, [(i, i ^ 1 << stride) for i in range(lax.axis_s...]
    ppermute x17, starting transfers between devices: 20.5 us -> 16.3 us  [swapped(): lax.ppermute(shard, axis, [(i, i ^ 1 << stride) for i in range(lax.axis_s...]
    pallas_call x1, Pallas kernels: 22.9 us -> 20 us  [shards(): pl.pallas_call(leaf_kernel, out_shape=(near(R, R), near(R, 2 * R), near(R...]
    pallas_call x5, Pallas kernels: 22.5 us -> 20.5 us  [invert(): pl.pallas_call(functools.partial(invert_kernel, level, levels), out_shape...]
    pallas_call x12 -> x9, Pallas kernels: 11.1 us -> 10.8 us  [condense(): pl.pallas_call(functools.partial(condense_kernel, level, levels, group),...]
  transfers between devices with their start and end apart: 17 -> 17, of which waited for: 6 -> 9; matrix products, arithmetic and copies ran while one was open for 0% -> 0% of each run, Pallas kernels for 27% -> 17%
where the time goes in v3:
time: 112 us; the launch traced here: 111 us
  Pallas kernels  54.9 us (49%)
  waiting for transfers between devices  39.2 us (35%)
  starting transfers between devices  16.3 us (15%)
    ppermute x17, waiting for transfers between devices, swapped(): lax.ppermute(shard, axis, [(i, i ^ 1 << stride) for i in range(lax.axis_s...  39.2 us
    pallas_call x5, Pallas kernels, invert(): pl.pallas_call(functools.partial(invert_kernel, level, levels), out_shape...  20.5 us
    pallas_call x1, Pallas kernels, shards(): pl.pallas_call(leaf_kernel, out_shape=(near(R, R), near(R, 2 * R), near(R...  20 us
    ppermute x17, starting transfers between devices, swapped(): lax.ppermute(shard, axis, [(i, i ^ 1 << stride) for i in range(lax.axis_s...  16.3 us
    pallas_call x9, Pallas kernels, condense(): pl.pallas_call(functools.partial(condense_kernel, level, levels, group),...  10.8 us
    pallas_call x1, Pallas kernels, shards(): pl.pallas_call(functools.partial(finish_kernel, levels), out_shape=f32(sl...  3.64 us
  transfers between devices with their start and end apart: 17, of which 9 were waited for; matrix products, arithmetic and copies ran while one was open for 0% of the time, Pallas kernels for 17%

profile of v3, /device:TPU:0, one launch (start us, length us, event | category | flops | bytes accessed | tf_op | source)
XLA Modules:
  0.0 111.3 jit_solution(18244028439400488331)
XLA Ops:
  0.8 20.0 %leaf.1 = (f32[128,128]{1,0:T(8,128)S(1)}, f32[128,256]{1,0:T(8,128)S(1)}, f32[128,2176]{1,0:T(8,128)S(1)}, f32[1024,1024]{1,0:T(8,128)S(1)}, f32[768,1024]{1,0:T(8,128)S(1)}) custom-call(s32[1]{0:T(128)S(6)} %copy.7.count_ref, f32[3,1024]{1,0:T(4,128)} %points_ref.1, s32[1,1024]{1,0:T(1,128)} %order_ref.1, f32[1024,640]{1,0:T(8,128)} %basis_ref.1, ...), custom_call_target="tpu_custom_call" | custom-call | tf_op jit(solution)/shard_map/leaf/pallas_call | solution.py:342
  21.4 2.4 %collective-permute-done.1.refs_0_ = f32[128,128]{1,0:T(8,128)S(1)} collective-permute-done((f32[128,128]{1,0:T(8,128)S(1)}, f32[128,128]{1,0:T(8,128)S(1)}, u32[]{:S(2)}, u32[]{:S(2)}) %collective-permute-start.1) | collective-permute-done | bytes 65568 | tf_op jit(solution)/shard_map/ppermute | solution.py:294
  23.9 3.4 %shard_map.64 = (f32[256,256]{1,0:T(8,128)S(1)}, f32[8,128]{1,0:T(8,128)S(1)}) custom-call(f32[128,128]{1,0:T(8,128)S(1)} %get-tuple-element.65.own_ref, f32[128,128]{1,0:T(8,128)S(1)} %collective-permute-done.1.refs_0_, f32[5,256,256]{2,1,0:T(8,128)S(1)} %copy-done, f32[8,128]{1,0:T(8,128)S(1)} %broadcast_in_dim.3.refs_2_), custom_call_target="tpu_custom_call" | custom-call | tf_op jit(solution)/shard_map/pallas_call | solution.py:379
  28.0 2.5 %shard_map.66 = (f32[128,256]{1,0:T(8,128)S(1)}, f32[128,384]{1,0:T(8,128)S(1)}, f32[128,1024]{1,0:T(8,128)S(1)}, f32[128,512]{1,0:T(8,128)S(1)}, f32[128,256]{1...) custom-call(f32[128,2176]{1,0:T(8,128)S(1)} %get-tuple-element.69.re, ...), custom_call_target="tpu_custom_call" | custom-call | tf_op jit(solution)/shard_map/pallas_call | solution.py:402
  30.5 2.9 %collective-permute-start.6 = (f32[128,512]{1,0:T(8,128)S(1)}, f32[128,512]{1,0:T(8,128)S(1)}, u32[]{:S(2)}, u32[]{:S(2)}) collective-permute-start(f32[128,512]{1,0:T(8,128)S(1)} %get-tuple-element.87), channel_id=1, source_target_pairs={{0,2},{1,3},{2,0},{3,1},{4,6},{5,7},{6,4},{7,5},{8,10},{9,11},{10,... | collective-permute-start | bytes 786440 | tf_op jit(solution)/shard_map/ppermute | solution.py:294
  33.4 6.8 %collective-permute-done.6.refs_1_ = f32[128,512]{1,0:T(8,128)S(1)} collective-permute-done((f32[128,512]{1,0:T(8,128)S(1)}, f32[128,512]{1,0:T(8,128)S(1)}, u32[]{:S(2)}, u32[]{:S(2)}) %collective-permute-start.6) | collective-permute-done | bytes 262176 | tf_op jit(solution)/shard_map/ppermute | solution.py:294
  40.2 1.7 %collective-permute-start.5 = (f32[128,384]{1,0:T(8,128)S(1)}, f32[128,384]{1,0:T(8,128)S(1)}, u32[]{:S(2)}, u32[]{:S(2)}) collective-permute-start(f32[128,384]{1,0:T(8,128)S(1)} %get-tuple-element.82.refs_0_), channel_id=1, source_target_pairs={{0,2},{1,3},{2,0},{3,1},{4,6},{5,7},{6,4},{7,5},{8,10},{9,11},{10,... | collective-permute-start | bytes 589832 | tf_op jit(solution)/shard_map/ppermute | solution.py:294
  42.3 1.7 %collective-permute-start.4 = (f32[128,128]{1,0:T(8,128)S(1)}, f32[128,128]{1,0:T(8,128)S(1)}, u32[]{:S(2)}, u32[]{:S(2)}) collective-permute-start(f32[128,128]{1,0:T(8,128)S(1)} %get-tuple-element.77.own_ref), channel_id=1, source_target_pairs={{0,2},{1,3},{2,0},{3,1},{4,6},{5,7},{6,4},{7,5},{8,10},{9,11},{10,... | collective-permute-start | bytes 196616 | tf_op jit(solution)/shard_map/ppermute | solution.py:294
  44.0 7.8 %collective-permute-done.4.refs_0_ = f32[128,128]{1,0:T(8,128)S(1)} collective-permute-done((f32[128,128]{1,0:T(8,128)S(1)}, f32[128,128]{1,0:T(8,128)S(1)}, u32[]{:S(2)}, u32[]{:S(2)}) %collective-permute-start.4) | collective-permute-done | bytes 65568 | tf_op jit(solution)/shard_map/ppermute | solution.py:294
  51.8 3.9 %shard_map.67 = (f32[256,256]{1,0:T(8,128)S(1)}, f32[8,128]{1,0:T(8,128)S(1)}) custom-call(f32[128,128]{1,0:T(8,128)S(1)} %get-tuple-element.77.own_ref, f32[128,128]{1,0:T(8,128)S(1)} %collective-permute-done.4.refs_0_, f32[5,256,256]{2,1,0:T(8,128)S(1)} %copy-done, f32[8,128]{1,0:T(8,128)S(1)} %get-tuple-element.78.refs_2_), custom_call_target="tpu_custom_call" | custom-call | tf_op jit(solution)/shard_map/pallas_call | solution.py:379
  57.1 1.7 %shard_map.70 = (f32[128,768]{1,0:T(8,128)S(1)}, f32[128,384]{1,0:T(8,128)S(1)}, f32[128,256]{1,0:T(8,128)}, f32[128,256]{1,0:T(8,128)}, f32[128,128]{1,0:T(8,12...) custom-call(f32[128,1024]{1,0:T(8,128)S(1)} %get-tuple-element.86.refs_0_, ...), custom_call_target="tpu_custom_call" | custom-call | tf_op jit(solution)/shard_map/pallas_call | solution.py:402
  60.1 5.1 %collective-permute-done.10.refs_1_ = f32[128,384]{1,0:T(8,128)S(1)} collective-permute-done((f32[128,384]{1,0:T(8,128)S(1)}, f32[128,384]{1,0:T(8,128)S(1)}, u32[]{:S(2)}, u32[]{:S(2)}) %collective-permute-start.10) | collective-permute-done | bytes 196640 | tf_op jit(solution)/shard_map/ppermute | solution.py:294
  65.2 1.3 %collective-permute-start.8 = (f32[128,256]{1,0:T(8,128)S(1)}, f32[128,256]{1,0:T(8,128)S(1)}, u32[]{:S(2)}, u32[]{:S(2)}) collective-permute-start(f32[128,256]{1,0:T(8,128)S(1)} %get-tuple-element.92.refs_0_), channel_id=1, source_target_pairs={{0,4},{4,0},{8,12},{12,8},{16,20},{20,16},{24,28},{28,24},{1,5},{5... | collective-permute-start | bytes 393224 | tf_op jit(solution)/shard_map/ppermute | solution.py:294
  67.2 5.3 %collective-permute-done.9.refs_0_ = f32[128,128]{1,0:T(8,128)S(1)} collective-permute-done((f32[128,128]{1,0:T(8,128)S(1)}, f32[128,128]{1,0:T(8,128)S(1)}, u32[]{:S(2)}, u32[]{:S(2)}) %collective-permute-start.9) | collective-permute-done | bytes 65568 | tf_op jit(solution)/shard_map/ppermute | solution.py:294
  72.5 4.1 %shard_map.71 = (f32[256,256]{1,0:T(8,128)S(1)}, f32[8,128]{1,0:T(8,128)S(1)}) custom-call(f32[128,128]{1,0:T(8,128)S(1)} %get-tuple-element.93.own_ref, f32[128,128]{1,0:T(8,128)S(1)} %collective-permute-done.9.refs_0_, f32[5,256,256]{2,1,0:T(8,128)S(1)} %copy-done, f32[8,128]{1,0:T(8,128)S(1)} %get-tuple-element.94.refs_2_), custom_call_target="tpu_custom_call" | custom-call | tf_op jit(solution)/shard_map/pallas_call | solution.py:379
  77.3 1.5 %shard_map.73 = (f32[128,512]{1,0:T(8,128)S(1)}, f32[128,256]{1,0:T(8,128)S(1)}, f32[128,256]{1,0:T(8,128)}, f32[128,256]{1,0:T(8,128)}, f32[128,128]{1,0:T(8,12...) custom-call(f32[128,768]{1,0:T(8,128)S(1)} %get-tuple-element.98.refs_0_, ...), custom_call_target="tpu_custom_call" | custom-call | tf_op jit(solution)/shard_map/pallas_call | solution.py:402
  80.0 3.8 %collective-permute-done.12.refs_1_ = f32[128,256]{1,0:T(8,128)S(1)} collective-permute-done((f32[128,256]{1,0:T(8,128)S(1)}, f32[128,256]{1,0:T(8,128)S(1)}, u32[]{:S(2)}, u32[]{:S(2)}) %collective-permute-start.12) | collective-permute-done | bytes 131104 | tf_op jit(solution)/shard_map/ppermute | solution.py:294
  85.0 3.3 %collective-permute-done.14.refs_0_ = f32[128,128]{1,0:T(8,128)S(1)} collective-permute-done((f32[128,128]{1,0:T(8,128)S(1)}, f32[128,128]{1,0:T(8,128)S(1)}, u32[]{:S(2)}, u32[]{:S(2)}) %collective-permute-start.14) | collective-permute-done | bytes 65568 | tf_op jit(solution)/shard_map/ppermute | solution.py:294
  88.3 4.3 %shard_map.74 = (f32[256,256]{1,0:T(8,128)S(1)}, f32[8,128]{1,0:T(8,128)S(1)}) custom-call(f32[128,128]{1,0:T(8,128)S(1)} %get-tuple-element.106.own_ref, f32[128,128]{1,0:T(8,128)S(1)} %collective-permute-done.14.refs_0_, f32[5,256,256]{2,1,0:T(8,128)S(1)} %copy-done, f32[8,128]{1,0:T(8,128)S(1)} %get-tuple-element.107.refs_2_), custom_call_target="tpu_custom_call" | custom-call | tf_op jit(solution)/shard_map/pallas_call | solution.py:379
  92.7 1.4 %shard_map.75 = (f32[128,128]{1,0:T(8,128)S(1)}, f32[128,128]{1,0:T(8,128)S(1)}, f32[128,128]{1,0:T(8,128)S(1)}, f32[128,256]{1,0:T(8,128)}, f32[128,256]{1,0:T(...) custom-call(f32[128,512]{1,0:T(8,128)S(1)} %get-tuple-element.104.refs_0_, ...), custom_call_target="tpu_custom_call" | custom-call | tf_op jit(solution)/shard_map/pallas_call | solution.py:402
  94.1 3.1 %collective-permute-start.15 = (f32[128,128]{1,0:T(8,128)S(1)}, f32[128,128]{1,0:T(8,128)S(1)}, u32[]{:S(2)}, u32[]{:S(2)}) collective-permute-start(f32[128,128]{1,0:T(8,128)S(1)} %get-tuple-element.113), channel_id=1, source_target_pairs={{0,16},{4,20},{8,24},{12,28},{16,0},{20,4},{24,8},{28,12},{1,17},{... | collective-permute-start | bytes 196616 | tf_op jit(solution)/shard_map/ppermute | solution.py:294
  97.2 3.4 %collective-permute-done.15.refs_0_.refs_1_ = f32[128,128]{1,0:T(8,128)S(1)} collective-permute-done((f32[128,128]{1,0:T(8,128)S(1)}, f32[128,128]{1,0:T(8,128)S(1)}, u32[]{:S(2)}, u32[]{:S(2)}) %collective-permute-start.15) | collective-permute-done | bytes 65568 | tf_op jit(solution)/shard_map/ppermute | solution.py:294
  101.8 4.8 %shard_map.76 = (f32[256,256]{1,0:T(8,128)S(1)}, f32[8,128]{1,0:T(8,128)S(1)}) custom-call(f32[128,128]{1,0:T(8,128)S(1)} %get-tuple-element.114.own_ref, f32[128,128]{1,0:T(8,128)S(1)} %collective-permute-done.15.refs_0_.refs_1_, f32[128,128]{1,0:T(8,128)S(1)} %collective-permute-done.16.refs_1_.refs_2_, f32[5,256,256]{2,1,0:T(8,128)S(1)} %copy-done, ...), custom_call_target="tpu_custom_call" | custom-call | tf_op jit(solution)/shard_map/pallas_call | solution.py:379
  107.6 3.6 %finish.1 = f32[1024,128]{1,0:T(8,128)} custom-call(f32[768,1024]{1,0:T(8,128)S(1)} %get-tuple-element.62.rows_ref, f32[1024,1024]{1,0:T(8,128)S(1)} %get-tuple-element.63.factor_ref, f32[128,128]{1,0:T(8,128)S(1)} %get-tuple-element.68.refs_0_, f32[128,128]{1,0:T(8,128)S(1)} %get-tuple-element.72.refs_1_, f32[128,128]{1,0:T(8,128)S(1)} %get-tuple-element.73.refs_2_, ...), custom_call_target="tpu_custom_call" | custom-call | tf_op jit(solution)/shard_map/finish/pallas_call | solution.py:431
  (29 shorter events, 10.4 us)
Async XLA Ops:
  0.0 23.9 %copy-start = (f32[5,256,256]{2,1,0:T(8,128)S(1)}, f32[5,256,256]{2,1,0:T(8,128)}, u32[]{:S(2)}) copy-start(f32[5,256,256]{2,1,0:T(8,128)} %refs_4_.7) | copy-start | bytes 3932164
  20.8 7.2 %collective-permute-start.2 = (f32[128,2176]{1,0:T(8,128)S(1)}, f32[128,2176]{1,0:T(8,128)S(1)}, u32[]{:S(2)}, u32[]{:S(2)}) collective-permute-start(f32[128,2176]{1,0:T(8,128)S(1)} %get-tuple-element.69.refs_0_), channel_id=1, source_target_pairs={{0,1},{1,0},{2,3},{3,2},{4,5},{5,4},{6,7},{7,6},{8,9},{9,8},{10,11... | collective-permute-start | bytes 3342344 | tf_op jit(solution)/shard_map/ppermute | solution.py:294
  20.9 6.4 %collective-permute-start = (f32[128,256]{1,0:T(8,128)S(1)}, f32[128,256]{1,0:T(8,128)S(1)}, u32[]{:S(2)}, u32[]{:S(2)}) collective-permute-start(f32[128,256]{1,0:T(8,128)S(1)} %get-tuple-element.64.refs_0_), channel_id=1, source_target_pairs={{0,1},{1,0},{2,3},{3,2},{4,5},{5,4},{6,7},{7,6},{8,9},{9,8},{10,11... | collective-permute-start | bytes 393224 | tf_op jit(solution)/shard_map/ppermute | solution.py:294
  21.4 2.5 %collective-permute-start.1 = (f32[128,128]{1,0:T(8,128)S(1)}, f32[128,128]{1,0:T(8,128)S(1)}, u32[]{:S(2)}, u32[]{:S(2)}) collective-permute-start(f32[128,128]{1,0:T(8,128)S(1)} %get-tuple-element.65.own_ref), channel_id=1, source_target_pairs={{0,1},{1,0},{2,3},{3,2},{4,5},{5,4},{6,7},{7,6},{8,9},{9,8},{10,11... | collective-permute-start | bytes 196616 | tf_op jit(solution)/shard_map/ppermute | solution.py:294
  30.5 9.7 %collective-permute-start.6 = (f32[128,512]{1,0:T(8,128)S(1)}, f32[128,512]{1,0:T(8,128)S(1)}, u32[]{:S(2)}, u32[]{:S(2)}) collective-permute-start(f32[128,512]{1,0:T(8,128)S(1)} %get-tuple-element.87), channel_id=1, source_target_pairs={{0,2},{1,3},{2,0},{3,1},{4,6},{5,7},{6,4},{7,5},{8,10},{9,11},{10,... | collective-permute-start | bytes 786440 | tf_op jit(solution)/shard_map/ppermute | solution.py:294
  40.2 16.8 %collective-permute-start.7 = (f32[128,512]{1,0:T(8,128)S(1)}, f32[128,512]{1,0:T(8,128)S(1)}, u32[]{:S(2)}, u32[]{:S(2)}) collective-permute-start(f32[128,512]{1,0:T(8,128)S(1)} %collective-permute-done.6.refs_1_), channel_id=1, source_target_pairs={{0,1},{1,0},{2,3},{3,2},{4,5},{5,4},{6,7},{7,6},{8,9},{9,8},{10,11... | collective-permute-start | bytes 786440 | tf_op jit(solution)/shard_map/ppermute | solution.py:294
  40.2 16.1 %collective-permute-start.5 = (f32[128,384]{1,0:T(8,128)S(1)}, f32[128,384]{1,0:T(8,128)S(1)}, u32[]{:S(2)}, u32[]{:S(2)}) collective-permute-start(f32[128,384]{1,0:T(8,128)S(1)} %get-tuple-element.82.refs_0_), channel_id=1, source_target_pairs={{0,2},{1,3},{2,0},{3,1},{4,6},{5,7},{6,4},{7,5},{8,10},{9,11},{10,... | collective-permute-start | bytes 589832 | tf_op jit(solution)/shard_map/ppermute | solution.py:294
  42.0 13.7 %collective-permute-start.3 = (f32[128,256]{1,0:T(8,128)S(1)}, f32[128,256]{1,0:T(8,128)S(1)}, u32[]{:S(2)}, u32[]{:S(2)}) collective-permute-start(f32[128,256]{1,0:T(8,128)S(1)} %get-tuple-element.76.refs_0_), channel_id=1, source_target_pairs={{0,2},{1,3},{2,0},{3,1},{4,6},{5,7},{6,4},{7,5},{8,10},{9,11},{10,... | collective-permute-start | bytes 393224 | tf_op jit(solution)/shard_map/ppermute | solution.py:294
  42.3 9.5 %collective-permute-start.4 = (f32[128,128]{1,0:T(8,128)S(1)}, f32[128,128]{1,0:T(8,128)S(1)}, u32[]{:S(2)}, u32[]{:S(2)}) collective-permute-start(f32[128,128]{1,0:T(8,128)S(1)} %get-tuple-element.77.own_ref), channel_id=1, source_target_pairs={{0,2},{1,3},{2,0},{3,1},{4,6},{5,7},{6,4},{7,5},{8,10},{9,11},{10,... | collective-permute-start | bytes 196616 | tf_op jit(solution)/shard_map/ppermute | solution.py:294
  58.7 6.5 %collective-permute-start.10 = (f32[128,384]{1,0:T(8,128)S(1)}, f32[128,384]{1,0:T(8,128)S(1)}, u32[]{:S(2)}, u32[]{:S(2)}) collective-permute-start(f32[128,384]{1,0:T(8,128)S(1)} %get-tuple-element.99), channel_id=1, source_target_pairs={{0,4},{4,0},{8,12},{12,8},{16,20},{20,16},{24,28},{28,24},{1,5},{5... | collective-permute-start | bytes 589832 | tf_op jit(solution)/shard_map/ppermute | solution.py:294
  65.2 12.1 %collective-permute-start.11 = (f32[128,384]{1,0:T(8,128)S(1)}, f32[128,384]{1,0:T(8,128)S(1)}, u32[]{:S(2)}, u32[]{:S(2)}) collective-permute-start(f32[128,384]{1,0:T(8,128)S(1)} %collective-permute-done.10.refs_1_), channel_id=1, source_target_pairs={{0,1},{1,0},{2,3},{3,2},{4,5},{5,4},{6,7},{7,6},{8,9},{9,8},{10,11... | collective-permute-start | bytes 589832 | tf_op jit(solution)/shard_map/ppermute | solution.py:294
  65.2 11.4 %collective-permute-start.8 = (f32[128,256]{1,0:T(8,128)S(1)}, f32[128,256]{1,0:T(8,128)S(1)}, u32[]{:S(2)}, u32[]{:S(2)}) collective-permute-start(f32[128,256]{1,0:T(8,128)S(1)} %get-tuple-element.92.refs_0_), channel_id=1, source_target_pairs={{0,4},{4,0},{8,12},{12,8},{16,20},{20,16},{24,28},{28,24},{1,5},{5... | collective-permute-start | bytes 393224 | tf_op jit(solution)/shard_map/ppermute | solution.py:294
  66.5 6.0 %collective-permute-start.9 = (f32[128,128]{1,0:T(8,128)S(1)}, f32[128,128]{1,0:T(8,128)S(1)}, u32[]{:S(2)}, u32[]{:S(2)}) collective-permute-start(f32[128,128]{1,0:T(8,128)S(1)} %get-tuple-element.93.own_ref), channel_id=1, source_target_pairs={{0,4},{4,0},{8,12},{12,8},{16,20},{20,16},{24,28},{28,24},{1,5},{5... | collective-permute-start | bytes 196616 | tf_op jit(solution)/shard_map/ppermute | solution.py:294
  78.8 5.1 %collective-permute-start.12 = (f32[128,256]{1,0:T(8,128)S(1)}, f32[128,256]{1,0:T(8,128)S(1)}, u32[]{:S(2)}, u32[]{:S(2)}) collective-permute-start(f32[128,256]{1,0:T(8,128)S(1)} %get-tuple-element.105), channel_id=1, source_target_pairs={{0,8},{4,12},{8,0},{12,4},{16,24},{20,28},{24,16},{28,20},{1,9},{5... | collective-permute-start | bytes 393224 | tf_op jit(solution)/shard_map/ppermute | solution.py:294
  83.8 8.8 %collective-permute-start.13 = (f32[128,256]{1,0:T(8,128)S(1)}, f32[128,256]{1,0:T(8,128)S(1)}, u32[]{:S(2)}, u32[]{:S(2)}) collective-permute-start(f32[128,256]{1,0:T(8,128)S(1)} %collective-permute-done.12.refs_1_), channel_id=1, source_target_pairs={{0,1},{1,0},{2,3},{3,2},{4,5},{5,4},{6,7},{7,6},{8,9},{9,8},{10,11... | collective-permute-start | bytes 393224 | tf_op jit(solution)/shard_map/ppermute | solution.py:294
  83.8 4.5 %collective-permute-start.14 = (f32[128,128]{1,0:T(8,128)S(1)}, f32[128,128]{1,0:T(8,128)S(1)}, u32[]{:S(2)}, u32[]{:S(2)}) collective-permute-start(f32[128,128]{1,0:T(8,128)S(1)} %get-tuple-element.106.own_ref), channel_id=1, source_target_pairs={{0,8},{4,12},{8,0},{12,4},{16,24},{20,28},{24,16},{28,20},{1,9},{5... | collective-permute-start | bytes 196616 | tf_op jit(solution)/shard_map/ppermute | solution.py:294
  94.1 6.5 %collective-permute-start.15 = (f32[128,128]{1,0:T(8,128)S(1)}, f32[128,128]{1,0:T(8,128)S(1)}, u32[]{:S(2)}, u32[]{:S(2)}) collective-permute-start(f32[128,128]{1,0:T(8,128)S(1)} %get-tuple-element.113), channel_id=1, source_target_pairs={{0,16},{4,20},{8,24},{12,28},{16,0},{20,4},{24,8},{28,12},{1,17},{... | collective-permute-start | bytes 196616 | tf_op jit(solution)/shard_map/ppermute | solution.py:294
  100.6 1.3 %collective-permute-start.16 = (f32[128,128]{1,0:T(8,128)S(1)}, f32[128,128]{1,0:T(8,128)S(1)}, u32[]{:S(2)}, u32[]{:S(2)}) collective-permute-start(f32[128,128]{1,0:T(8,128)S(1)} %collective-permute-done.15.refs_0_.refs_1_), channel_id=1, source_target_pairs={{0,1},{1,0},{2,3},{3,2},{4,5},{5,4},{6,7},{7,6},{8,9},{9,8},{10,11... | collective-permute-start | bytes 196616 | tf_op jit(solution)/shard_map/ppermute | solution.py:294
